TPU v7x, 32 devices: a whole 2x2x4 slice. The times are simulated.
32 devices in a mesh: dp: 4 (over y, core), code: 8 (over z, x).
Axes of the slice: x: 2, y: 2, z: 4, core: 2. Of those that a mesh axis runs over, the one named last changes fastest.
Arguments:
- cached_keys: bfloat16 [131072, 128], P(('dp', 'code')), may hold values from -128 to 128
- codebook: float32 [65536, 128], P('code'), may hold values from -4 to 4
- block_lists: int32 [256, 6], P(('dp', 'code')), may hold values from 0 to 255, as said below
- counts: int32 [256], P(('dp', 'code')), may hold values from 2 to 6, as said below
Outputs:
- codebook_out: float32 [65536, 128], P('code')
- logsum: float32 [131072], P(('dp', 'code'))
Inputs may be any that keep to these rules, and one draw needn't show every extreme that they name: `block_lists`: within a row the first counts entries are distinct; entries past the count repeat the first. Owner o holds blocks o * (256 / the size of code) onward, consecutively; the key blocks of one device (aligned runs of 8 rows) name at most 1 distinct blocks of one owner, and in every draw one owner has exactly 1 named by every device. `counts`: some key block of every device lists 6 blocks.
All inputs are finite; a program needn't handle non-finite values.
Results may differ from a plain program's by a relative error of at most 0.0007.
Values sent between devices are 32-bit elements; how exact they have to be, the bound alone decides.
A program may use at most 64 MiB of HBM per device.

v0:
```python
import math

import jax
import jax.numpy as jnp
from jax import lax
from jax.sharding import PartitionSpec as P

CBLK = 256
LIST_MAX = 6
CAP = 1
ITERS = 2


def on_device(cached_keys, codebook, block_lists, counts):
    masked_score = -1e30
    code_count = lax.axis_size("code")
    own_rows, feature = codebook.shape
    own_blocks = own_rows // CBLK
    slot_count = code_count * CAP
    key_blocks = block_lists.shape[0]
    all_blocks = own_blocks * code_count
    listed_ok = jnp.arange(LIST_MAX)[None, :] < counts[:, None]
    flat_ids = block_lists.reshape(-1)
    block_range = jnp.arange(all_blocks, dtype=jnp.int32)
    matches = flat_ids[:, None] == block_range[None, :]
    present = (
        jnp.any(matches & listed_ok.reshape(-1)[:, None], axis=0)
        .astype(jnp.int32)
        .reshape(code_count, own_blocks)
    )
    before = jnp.cumsum(present, axis=1) - present
    chosen = present[:, :, None] * (
        before[:, :, None] == jnp.arange(CAP, dtype=jnp.int32)[None, None, :]
    ).astype(jnp.int32)
    wanted = jnp.sum(chosen * jnp.arange(own_blocks, dtype=jnp.int32)[None, :, None], axis=1)
    entry_rank = jnp.sum(matches.astype(jnp.int32) * before.reshape(-1)[None, :], axis=1)
    entry_slot = (flat_ids // own_blocks * CAP + entry_rank).reshape(key_blocks, LIST_MAX)
    block_keys = cached_keys.reshape(key_blocks, -1, feature)
    inv_scale = 1.0 / math.sqrt(feature)
    current = codebook
    logsum = None
    for sweep in range(ITERS):
        code_full = current.reshape(own_blocks, CBLK, feature)
        code_norm = jnp.sum(current * current, axis=1).reshape(own_blocks, CBLK)

        def serve_blocks(requested, code_full=code_full, code_norm=code_norm):
            served = code_full[requested]
            served_norm = code_norm[requested]
            back_words, back_norms = (
                lax.all_to_all(served, "code", split_axis=0, concat_axis=0, tiled=True),
                lax.all_to_all(served_norm, "code", split_axis=0, concat_axis=0, tiled=True),
            )
            return (back_words, back_norms, requested)

        fetched, fetched_norm, requested = serve_blocks(
            lax.all_to_all(wanted, "code", split_axis=0, concat_axis=0, tiled=True)
        )
        fetched = fetched.reshape(slot_count, CBLK, feature)
        fetched_norm = fetched_norm.reshape(slot_count, CBLK)

        def one_block(running, block_item):
            slot_sums, slot_mass = running
            tile_keys, slot_picks, listed = block_item
            word_rows = fetched[slot_picks].reshape(-1, feature)
            word_norms = fetched_norm[slot_picks].reshape(-1)
            inner = lax.dot_general(
                tile_keys.astype(jnp.float32),
                word_rows,
                (((1,), (1,)), ((), ())),
                precision=lax.Precision.HIGHEST,
                preferred_element_type=jnp.float32,
            )
            scores = (inner - 0.5 * word_norms[None, :]) * inv_scale
            column_live = jnp.repeat(listed, CBLK)
            scores = jnp.where(column_live[None, :], scores, masked_score)
            row_top = jnp.max(scores, axis=1, keepdims=True)
            unnorm = jnp.exp(scores - row_top)
            row_total = jnp.sum(unnorm, axis=1, keepdims=True)
            row_logsum = row_top[:, 0] + jnp.log(row_total[:, 0])
            posterior = (unnorm / row_total).astype(jnp.bfloat16)
            weighted = lax.dot_general(
                posterior, tile_keys, (((0,), (0,)), ((), ())), preferred_element_type=jnp.float32
            )
            weight = jnp.sum(posterior.astype(jnp.float32), axis=0)
            slot_sums = slot_sums.at[slot_picks].add(weighted.reshape(LIST_MAX, CBLK, feature))
            slot_mass = slot_mass.at[slot_picks].add(weight.reshape(LIST_MAX, CBLK))
            return ((slot_sums, slot_mass), row_logsum)

        start_state = (
            jnp.zeros((slot_count, CBLK, feature), jnp.float32),
            jnp.zeros((slot_count, CBLK), jnp.float32),
        )
        (slot_sums, slot_mass), logsum = lax.scan(
            one_block, start_state, (block_keys, entry_slot, listed_ok)
        )
        arrived, arrived_mass = (
            lax.all_to_all(
                slot_sums.reshape(code_count, CAP, CBLK, feature),
                "code",
                split_axis=0,
                concat_axis=0,
                tiled=True,
            ),
            lax.all_to_all(
                slot_mass.reshape(code_count, CAP, CBLK),
                "code",
                split_axis=0,
                concat_axis=0,
                tiled=True,
            ),
        )
        owner_index = requested.reshape(-1)
        owner_sums = (
            jnp.zeros((own_blocks, CBLK, feature), jnp.float32)
            .at[owner_index]
            .add(arrived.reshape(-1, CBLK, feature))
        )
        owner_mass = (
            jnp.zeros((own_blocks, CBLK), jnp.float32)
            .at[owner_index]
            .add(arrived_mass.reshape(-1, CBLK))
        )
        owner_sums = owner_sums.reshape(own_rows, feature)
        owner_mass = owner_mass.reshape(own_rows)
        share_rows = own_rows // lax.axis_size("dp")
        part_sum, part_mass = (
            lax.psum_scatter(owner_sums, "dp", scatter_dimension=0, tiled=True),
            lax.psum_scatter(owner_mass, "dp", scatter_dimension=0, tiled=True),
        )
        first_row = lax.axis_index("dp") * share_rows
        previous = lax.dynamic_slice_in_dim(current, first_row, share_rows, 0)
        updated = (part_sum + previous) / (part_mass[:, None] + 1.0)
        current = lax.all_gather(updated, "dp", axis=0, tiled=True)
    return (current, logsum.reshape(-1))


def solution(mesh):
    in_specs = (
        P(("dp", "code"), None),
        P("code", None),
        P(("dp", "code"), None),
        P(("dp", "code")),
    )
    out_specs = (P("code", None), P(("dp", "code")))
    return jax.shard_map(
        on_device, mesh=mesh, in_specs=in_specs, out_specs=out_specs, check_vma=False
    )
```

profile of v0, /device:TPU:0, one launch (start us, length us, event | category | flops | bytes accessed | tf_op | source)
XLA Modules:
  0.0 557.2 jit_solution(14264535916855400787)
XLA Ops:
  9.9 7.3 %all-to-all-start = ((s32[8,1,1]{2,1,0:T(1,128)}), s32[8,1,1]{2,1,0:T(1,128)S(1)}, u32[]{:S(2)}, u32[]{:S(2)}) async-start(s32[8,1,1]{2,1,0:T(1,128)} %copy.22), calls=%async_computation | async-start | bytes 8192 | tf_op jit(solution)/shard_map/all_to_all | solution.py:56
  17.2 3.3 multiply_reduce_fusion.1
  28.5 3.8 gather_fusion.4
  35.0 4.2 all-to-all-start.1
  39.6 23.5 %all-to-all-done.1 = f32[8,1,256,128]{3,2,1,0:T(8,128)} async-done(((f32[8,1,256,128]{3,2,1,0:T(8,128)}), f32[8,1,256,128]{3,2,1,0:T(8,128)}, u32[]{:S(2)}, u32[]{:S(2)}) %all-to-all-start.1) | async-done | bytes 1048608 | tf_op jit(solution)/shard_map/all_to_all | solution.py:50
  64.2 101.4 %while.26 = (s32[]{:T(128)}, f32[8,256,128]{2,1,0:T(8,128)}, f32[8,256]{1,0:T(8,128)S(1)}, s32[8,6]{1,0:T(8,128)S(1)}, pred[8,6]{1,0:T(8,128)(4,1)S(1)}, /*index...) while((s32[]{:T(128)}, f32[8,256,128]{2,1,0:T(8,128)}, ...), condition=%wide.region_11.12_spmd, body=%wide.region_5.11_spmd.sunk | while | flops 1418135040 | bytes 21596464 | solution.py:93
  165.6 3.6 all-to-all-start.3
  169.2 25.5 %all-to-all-done.3 = f32[8,1,256,128]{3,2,1,0:T(8,128)S(1)} async-done(((f32[8,1,256,128]{3,2,1,0:T(8,128)}), f32[8,1,256,128]{3,2,1,0:T(8,128)S(1)}, u32[]{:S(2)}, u32[]{:S(2)}) %all-to-all-start.3) | async-done | bytes 1048608 | tf_op jit(solution)/shard_map/all_to_all | solution.py:97
  201.2 3.5 all-to-all-start.4
  206.1 5.1 all-to-all-done.4
  211.9 10.8 %all-reduce = f32[8192]{0:T(1024)S(1)} all-reduce(f32[8192]{0:T(1024)S(1)} %bitcast.147), channel_id=3, replica_groups=mesh['dp'=4,'code'=8] {'dp'}, use_global_device_ids=true, to_apply=%region_15.16.clone | all-reduce | flops 8192 | bytes 65536
  222.7 21.5 %reduce-scatter.3.cloned.1.call-done = f32[2048,128]{1,0:T(8,128)} async-done(((f32[8192,128]{1,0:T(8,128)}), f32[2048,128]{1,0:T(8,128)}) %reduce-scatter.3.cloned.1.call-update) | async-done | bytes 1048592 | tf_op jit(solution)/shard_map/reduce_scatter | solution.py:127
  247.0 34.4 %all-gather.3.cloned.1.call-done = f32[8192,128]{1,0:T(8,128)} async-done(((f32[2048,128]{1,0:T(8,128)}), f32[8192,128]{1,0:T(8,128)}) %all-gather.3.cloned.1.call-update) | async-done | bytes 4194320 | tf_op jit(solution)/shard_map/all_gather | solution.py:133
  286.0 5.5 all-to-all-start.6
  291.5 3.8 gather_fusion.6
  298.1 4.2 all-to-all-start.5
  302.6 25.0 %all-to-all-done.5 = f32[8,1,256,128]{3,2,1,0:T(8,128)} async-done(((f32[8,1,256,128]{3,2,1,0:T(8,128)}), f32[8,1,256,128]{3,2,1,0:T(8,128)}, u32[]{:S(2)}, u32[]{:S(2)}) %all-to-all-start.5) | async-done | bytes 1048608 | tf_op jit(solution)/shard_map/all_to_all | solution.py:50
  328.6 102.0 %while.27 = (s32[]{:T(128)}, f32[8,256,128]{2,1,0:T(8,128)}, f32[8,256]{1,0:T(8,128)S(1)}, f32[8,512]{1,0:T(8,128)S(1)}, s32[8,6]{1,0:T(8,128)S(1)}, /*index=5*/...) while((s32[]{:T(128)}, f32[8,256,128]{2,1,0:T(8,128)}, ...), condition=%wide.region_23.24_spmd, body=%wide.region_17.23_spmd.sunk | while | flops 1418135552 | bytes 21606724 | solution.py:93
  430.6 29.4 %all_to_all.53 = f32[8,1,256,128]{3,2,1,0:T(8,128)S(1)} all-to-all(f32[8,1,256,128]{3,2,1,0:T(8,128)} %bitcast.134), channel_id=1, replica_groups=mesh['dp'=4,'code'=8] {'code'}, dimensions={0} | all-to-all | bytes 2097152 | tf_op jit(solution)/shard_map/all_to_all | solution.py:97
  465.9 10.0 %all_to_all.54 = f32[8,1,256]{2,1,0:T(1,128)S(1)} all-to-all(f32[8,1,256]{2,1,0:T(1,128)S(1)} %reshape.304), channel_id=1, replica_groups=mesh['dp'=4,'code'=8] {'code'}, dimensions={0} | all-to-all | bytes 16384 | tf_op jit(solution)/shard_map/all_to_all | solution.py:104
  476.5 10.9 %all-reduce.1 = f32[8192]{0:T(1024)S(1)} all-reduce(f32[8192]{0:T(1024)S(1)} %bitcast.148), channel_id=5, replica_groups=mesh['dp'=4,'code'=8] {'dp'}, use_global_device_ids=true, to_apply=%region_27.28.clone | all-reduce | flops 8192 | bytes 65536
  487.5 21.3 %reduce-scatter.5.cloned.1.call-done = f32[2048,128]{1,0:T(8,128)} async-done(((f32[8192,128]{1,0:T(8,128)}), f32[2048,128]{1,0:T(8,128)}) %reduce-scatter.5.cloned.1.call-update) | async-done | bytes 1048592 | tf_op jit(solution)/shard_map/reduce_scatter | solution.py:127
  512.3 33.9 %all-gather.5.cloned.1.call-done = f32[8192,128]{1,0:T(8,128)} async-done(((f32[2048,128]{1,0:T(8,128)}), f32[8192,128]{1,0:T(8,128)}) %all-gather.5.cloned.1.call-update) | async-done | bytes 4194320 | tf_op jit(solution)/shard_map/all_gather | solution.py:133
  546.2 4.5 copy.79
  (351 shorter events, 246.2 us)
Async XLA Ops:
  9.9 13.7 %all-to-all-start = ((s32[8,1,1]{2,1,0:T(1,128)}), s32[8,1,1]{2,1,0:T(1,128)S(1)}, u32[]{:S(2)}, u32[]{:S(2)}) async-start(s32[8,1,1]{2,1,0:T(1,128)} %copy.22), calls=%async_computation | async-start | bytes 8192 | tf_op jit(solution)/shard_map/all_to_all | solution.py:56
  20.6 19.0 %copy-start = (s32[8,6]{1,0:T(8,128)S(1)}, s32[8,6]{1,0:T(8,128)}, u32[]{:S(2)}) copy-start(s32[8,6]{1,0:T(8,128)} %param.10) | copy-start | bytes 580
  25.2 9.8 %all-to-all-start.2 = ((f32[8,1,256]{2,1,0:T(1,128)}), f32[8,1,256]{2,1,0:T(1,128)S(1)}, u32[]{:S(2)}, u32[]{:S(2)}) async-start(f32[8,1,256]{2,1,0:T(1,128)} %copy.23), calls=%async_computation.2 | async-start | bytes 16384 | tf_op jit(solution)/shard_map/all_to_all | solution.py:51
  35.0 28.2 %all-to-all-start.1 = ((f32[8,1,256,128]{3,2,1,0:T(8,128)}), f32[8,1,256,128]{3,2,1,0:T(8,128)}, u32[]{:S(2)}, u32[]{:S(2)}) async-start(f32[8,1,256,128]{3,2,1,0:T(8,128)} %bitcast.21), calls=%async_computation.1 | async-start | bytes 2097152 | tf_op jit(solution)/shard_map/all_to_all | solution.py:50
  165.6 29.1 %all-to-all-start.3 = ((f32[8,1,256,128]{3,2,1,0:T(8,128)}), f32[8,1,256,128]{3,2,1,0:T(8,128)S(1)}, u32[]{:S(2)}, u32[]{:S(2)}) async-start(f32[8,1,256,128]{3,2,1,0:T(8,128)} %bitcast.135), calls=%async_computation.3 | async-start | bytes 2097152 | tf_op jit(solution)/shard_map/all_to_all | solution.py:97
  169.2 75.0 %reduce-scatter.3.cloned.1.call-start = ((), (), s32[]{:S(2)}) async-start(), calls=%async_computation.11 | async-start | bytes 5242880 | tf_op jit(solution)/shard_map/reduce_scatter | solution.py:127
  197.2 7.5 %copy-start.1 = (u32[32]{0:T(128)S(1)}, u32[32]{0:T(128)}, u32[]{:S(2)}) copy-start(u32[32]{0:T(128)} %constant.99) | copy-start | bytes 388
  201.2 10.0 %all-to-all-start.4 = ((f32[8,1,256]{2,1,0:T(1,128)}), f32[8,1,256]{2,1,0:T(1,128)S(1)}, u32[]{:S(2)}, u32[]{:S(2)}) async-start(f32[8,1,256]{2,1,0:T(1,128)} %reshape.294), calls=%async_computation.5 | async-start | bytes 16384 | tf_op jit(solution)/shard_map/all_to_all | solution.py:104
  204.7 76.8 %all-gather.3.cloned.1.call-start = ((), (), s32[]{:S(2)}) async-start(), calls=%async_computation.12 | async-start | bytes 5242880 | tf_op jit(solution)/shard_map/all_gather | solution.py:133
  286.0 12.0 %all-to-all-start.6 = ((f32[8,1,256]{2,1,0:T(1,128)}), f32[8,1,256]{2,1,0:T(1,128)S(1)}, u32[]{:S(2)}, u32[]{:S(2)}) async-start(f32[8,1,256]{2,1,0:T(1,128)} %copy.24), calls=%async_computation.7 | async-start | bytes 16384 | tf_op jit(solution)/shard_map/all_to_all | solution.py:51
  298.1 29.4 %all-to-all-start.5 = ((f32[8,1,256,128]{3,2,1,0:T(8,128)}), f32[8,1,256,128]{3,2,1,0:T(8,128)}, u32[]{:S(2)}, u32[]{:S(2)}) async-start(f32[8,1,256,128]{3,2,1,0:T(8,128)} %bitcast.28), calls=%async_computation.6 | async-start | bytes 2097152 | tf_op jit(solution)/shard_map/all_to_all | solution.py:50
  302.3 206.5 %reduce-scatter.5.cloned.1.call-start = ((), (), s32[]{:S(2)}) async-start(), calls=%async_computation.13 | async-start | bytes 5242880 | tf_op jit(solution)/shard_map/reduce_scatter | solution.py:127
  465.8 80.4 %all-gather.5.cloned.1.call-start = ((), (), s32[]{:S(2)}) async-start(), calls=%async_computation.14 | async-start | bytes 5242880 | tf_op jit(solution)/shard_map/all_gather | solution.py:133
Sparse Core Ops, SparseCore 0:
  200.7 43.4 reduce-scatter.2
  247.2 34.2 all-gather.2
  466.0 42.7 reduce-scatter.4
  511.8 34.3 all-gather.4
where the time goes:
time: 560 us; the launch traced here: 557 us
  waiting for transfers between devices  199 us (36%)
  other arithmetic  104 us (19%)
  local copies, waits for them, and re-layouts  76.7 us (14%)
  matrix products  68.6 us (12%)
  blocking collectives  61.1 us (11%)
  starting transfers between devices  32 us (6%)
  between operations  14.7 us (3%)
    all_gather x2, waiting for transfers between devices, on_device(): current = lax.all_gather(updated, 'dp', axis=0, tiled=True)  68.4 us
    scatter-add x16, other arithmetic, one_block(): slot_sums.at[slot_picks].add(weighted.reshape(LIST_MAX, CBLK, feature))  48.6 us
    all_to_all x2, waiting for transfers between devices, serve_blocks(): lax.all_to_all(served, 'code', split_axis=0, concat_axis=0, tiled=True)  48.5 us
    dot_general x16, matrix products, one_block(): lax.dot_general(tile_keys.astype(jnp.float32), word_rows, (((1,), (1,)),...  45 us
    reduce_scatter x2, waiting for transfers between devices, on_device(): lax.psum_scatter(owner_sums, 'dp', scatter_dimension=0, tiled=True)  42.7 us
    all_to_all x1, blocking collectives, on_device(): lax.all_to_all(slot_sums.reshape(code_count, CAP, CBLK, feature), 'code',...  29.4 us
    gather x16, local copies, waits for them, and re-layouts, one_block(): word_rows = fetched[slot_picks].reshape(-1, feature)  29.1 us
    all_to_all x1, waiting for transfers between devices, on_device(): lax.all_to_all(slot_sums.reshape(code_count, CAP, CBLK, feature), 'code',...  25.5 us
  transfers between devices with their start and end apart: 11, of which 11 were waited for; matrix products, arithmetic and copies ran while one was open for 3% of the time, Pallas kernels for 0%

commit v1 on v0

v1 whole, which is shorter than its diff:
```python
import functools
import math

import jax
import jax.numpy as jnp
from jax import lax
from jax.experimental import pallas as pl
from jax.experimental.pallas import tpu as pltpu
from jax.sharding import PartitionSpec as P

CBLK = 256
LIST_MAX = 6
ITERS = 2
MROWS = 8
MESH = pl.DeviceIdType.MESH
VLIMIT = 60 * 1024 * 1024

VM = pl.BlockSpec(memory_space=pltpu.VMEM)
SM = pl.BlockSpec(memory_space=pltpu.SMEM)


def ids_kernel(n_dp, n_code, want_ref, all_ref, send_sem, recv_sem):
    n = n_dp * n_code
    me = lax.axis_index("dp") * n_code + lax.axis_index("code")
    barrier = pltpu.get_barrier_semaphore()

    def greet(k, c):
        peer = (me + k) % n
        pl.semaphore_signal(
            barrier, inc=1, device_id=(peer // n_code, peer % n_code), device_id_type=MESH
        )
        return c

    lax.fori_loop(1, n, greet, 0)
    all_ref[me] = want_ref[...]
    pl.semaphore_wait(barrier, n - 1)

    def copy(k):
        peer = (me + k) % n
        return pltpu.make_async_remote_copy(
            src_ref=want_ref,
            dst_ref=all_ref.at[me],
            send_sem=send_sem.at[k],
            recv_sem=recv_sem.at[k],
            device_id=(peer // n_code, peer % n_code),
            device_id_type=MESH,
        )

    def start(k, c):
        copy(k).start()
        return c

    lax.fori_loop(1, n, start, 0)

    def finish(k, c):
        copy(k).wait()
        return c

    lax.fori_loop(1, n, finish, 0)


def fetch_kernel(n_code, ids_ref, book_ref, out_ref, stage, send_sem, recv_sem):
    d = lax.axis_index("dp")
    o = lax.axis_index("code")
    barrier = pltpu.get_barrier_semaphore()
    for k in range(1, n_code):
        pl.semaphore_signal(barrier, inc=1, device_id=(d, (o + k) % n_code), device_id_type=MESH)
    for k in range(n_code):
        peer = (o + k) % n_code
        block = book_ref[ids_ref[d * n_code + peer]]
        if k == 0:
            out_ref[o] = block
        else:
            stage[k] = block
    pl.semaphore_wait(barrier, n_code - 1)
    copies = []
    for k in range(1, n_code):
        copy = pltpu.make_async_remote_copy(
            src_ref=stage.at[k],
            dst_ref=out_ref.at[o],
            send_sem=send_sem.at[k],
            recv_sem=recv_sem.at[k],
            device_id=(d, (o + k) % n_code),
            device_id_type=MESH,
        )
        copy.start()
        copies.append(copy)
    for copy in copies:
        copy.wait()


def gather_kernel(
    n_dp, n_code, sums_ref, out_ref, a_send, a_recv, y_send, y_recv, c_send, c_recv, own_sem
):
    d = lax.axis_index("dp")
    o = lax.axis_index("code")
    n_y = n_dp // 2
    y = d // 2
    core = d % 2
    mate = y * 2 + 1 - core
    barrier = pltpu.get_barrier_semaphore()
    for k in range(1, n_code):
        pl.semaphore_signal(barrier, inc=1, device_id=(d, (o + k) % n_code), device_id_type=MESH)
    for j in range(1, n_y):
        pl.semaphore_signal(
            barrier, inc=1, device_id=((y + j) % n_y * 2 + core, o), device_id_type=MESH
        )
    pl.semaphore_signal(barrier, inc=1, device_id=(mate, o), device_id_type=MESH)
    own = pltpu.make_async_copy(sums_ref.at[o], out_ref.at[d * n_code + o], own_sem)
    own.start()
    pl.semaphore_wait(barrier, n_code - 1 + n_y - 1 + 1)

    waits = []
    across = []
    for k in range(1, n_code):
        copy = pltpu.make_async_remote_copy(
            src_ref=sums_ref.at[(o + k) % n_code],
            dst_ref=out_ref.at[d * n_code + o],
            send_sem=a_send.at[k],
            recv_sem=a_recv.at[k],
            device_id=(d, (o + k) % n_code),
            device_id_type=MESH,
        )
        copy.start()
        across.append(copy)
        waits.append(copy.wait_send)

    def to_y(k, j):
        row = d * n_code + (o + n_code - k) % n_code
        return pltpu.make_async_remote_copy(
            src_ref=out_ref.at[row],
            dst_ref=out_ref.at[row],
            send_sem=y_send.at[j, k],
            recv_sem=y_recv.at[j, k],
            device_id=((y + j) % n_y * 2 + core, o),
            device_id_type=MESH,
        )

    def to_mate(k, j):
        row = ((y + n_y - j) % n_y * 2 + core) * n_code + (o + n_code - k) % n_code
        return pltpu.make_async_remote_copy(
            src_ref=out_ref.at[row],
            dst_ref=out_ref.at[row],
            send_sem=c_send.at[j, k],
            recv_sem=c_recv.at[j, k],
            device_id=(mate, o),
            device_id_type=MESH,
        )

    y_copies = {}
    for k in range(n_code):
        if k == 0:
            own.wait()
        else:
            across[k - 1].wait_recv()
        for j in range(1, n_y):
            copy = to_y(k, j)
            copy.start()
            y_copies[j, k] = copy
            waits.append(copy.wait_send)
        copy = to_mate(k, 0)
        copy.start()
        waits.append(copy.wait_send)
        waits.append(copy.wait_recv)
    for k in range(n_code):
        for j in range(1, n_y):
            y_copies[j, k].wait_recv()
            copy = to_mate(k, j)
            copy.start()
            waits.append(copy.wait_send)
            waits.append(copy.wait_recv)
    for wait in waits:
        wait()


def update_kernel(n, own_blocks, ids_ref, con_ref, book_ref, out_ref, sums, mass):
    sums[...] = book_ref[...]
    mass[...] = jnp.ones_like(mass)

    def add(j, c):
        b = ids_ref[j]
        sums[b] += con_ref[j, :CBLK]
        mass[b] += con_ref[j, CBLK:]
        return c

    lax.fori_loop(0, n, add, 0)

    def finish(b, c):
        for h in range(2):
            inv = 1.0 / mass[b, pl.ds(h, 1), :]
            column = jnp.transpose(jnp.broadcast_to(inv, (128, 128)))
            rows = pl.ds(h * 128, 128)
            out_ref[b, rows, :] = sums[b, rows, :] * column
        return c

    lax.fori_loop(0, own_blocks, finish, 0)


def assign_kernel(
    n_slots, key_blocks, block, feature,
    slots_ref, counts_ref, fetched_ref, keys_ref,
    sums_ref, logsum_ref,
    words, kst, kext, scores, acc, top,
):
    inv_scale = 1.0 / math.sqrt(feature)
    log2e = math.log2(math.e)
    lane = lax.broadcasted_iota(jnp.int32, (CBLK, 128), 1)

    def split(value):
        hi = value.astype(jnp.bfloat16)
        rest = value - hi.astype(jnp.float32)
        mid = rest.astype(jnp.bfloat16)
        lo = (rest - mid.astype(jnp.float32)).astype(jnp.bfloat16)
        return hi, mid, lo

    def prepare(s, c):
        value = fetched_ref[s]
        hi, mid, lo = split(value)
        words[s, :, 0:128] = hi
        words[s, :, 128:256] = mid
        words[s, :, 256:384] = lo
        half = -0.5 * jnp.sum(value * value, axis=1, keepdims=True)
        n_hi, n_mid, n_lo = [t.astype(jnp.float32) for t in split(half)]
        extra = jnp.where(
            lane == 0, n_hi, jnp.where(lane == 1, n_mid, jnp.where(lane == 2, n_lo, 0.0))
        )
        words[s, :, 384:512] = extra.astype(jnp.bfloat16)
        acc[s] = jnp.zeros((CBLK, 256), jnp.float32)
        return c

    lax.fori_loop(0, n_slots, prepare, 0)
    kst[384:512, :] = jnp.ones((128, block), jnp.bfloat16)
    kext[:, 128:256] = jnp.ones((block, 128), jnp.bfloat16)

    def key_block(kb, c):
        keys = keys_ref[pl.ds(pl.multiple_of(kb * block, block), block), :]
        kext[:, 0:128] = keys
        turned = jnp.transpose(keys)
        kst[0:128, :] = turned
        kst[128:256, :] = turned
        kst[256:384, :] = turned
        count = counts_ref[kb]
        top[...] = jnp.full((8, block), -3e38, jnp.float32)

        def score(l, c2):
            s = jnp.dot(words[slots_ref[kb, l]], kst[...], preferred_element_type=jnp.float32)
            scores[l] = s
            top[...] = jnp.maximum(top[...], jnp.max(s.reshape(CBLK // 8, 8, block), axis=0))
            return c2

        lax.fori_loop(0, count, score, 0)
        peak = jnp.max(top[...], axis=0, keepdims=True)

        def expo(l, total):
            e = jnp.exp2((scores[l] - peak) * (inv_scale * log2e))
            scores[l] = e
            return total + jnp.sum(e.reshape(CBLK // 8, 8, block), axis=0)

        total = lax.fori_loop(0, count, expo, jnp.zeros((8, block), jnp.float32))
        total = jnp.sum(total, axis=0, keepdims=True)
        logsum_ref[kb] = peak * inv_scale + jnp.log(total)
        inv = 1.0 / total

        def spread(l, c2):
            p = (scores[l] * inv).astype(jnp.bfloat16)
            slot = slots_ref[kb, l]
            acc[slot] += jnp.dot(p, kext[...], preferred_element_type=jnp.float32)
            return c2

        lax.fori_loop(0, count, spread, 0)
        return c

    lax.fori_loop(0, key_blocks, key_block, 0)

    def write(s, c):
        sums_ref[s, :CBLK, :] = acc[s, :, 0:128]
        for h in range(2):
            turned = jnp.transpose(acc[s, pl.ds(h * 128, 128), pl.ds(128, 128)])
            sums_ref[s, pl.ds(CBLK + h, 1), :] = turned[0:1, :]
        sums_ref[s, CBLK + 2 :, :] = jnp.zeros((MROWS - 2, 128), jnp.float32)
        return c

    lax.fori_loop(0, n_slots, write, 0)


def on_device(cached_keys, codebook, block_lists, counts):
    n_dp = lax.axis_size("dp")
    n_code = lax.axis_size("code")
    n = n_dp * n_code
    own_rows, feature = codebook.shape
    own_blocks = own_rows // CBLK
    key_blocks = block_lists.shape[0]
    block = cached_keys.shape[0] // key_blocks
    f32 = jnp.float32
    dma = pltpu.SemaphoreType.DMA

    slots = block_lists // own_blocks
    local = block_lists % own_blocks
    wanted = jnp.max(
        jnp.where(
            slots.reshape(-1)[:, None] == jnp.arange(128)[None, :], local.reshape(-1)[:, None], 0
        ),
        axis=0,
    )
    everyone = pl.pallas_call(
        functools.partial(ids_kernel, n_dp, n_code),
        out_shape=jax.ShapeDtypeStruct((n, 8, 128), jnp.int32),
        in_specs=[VM],
        out_specs=VM,
        scratch_shapes=[dma((n,)), dma((n,))],
        compiler_params=pltpu.CompilerParams(collective_id=0, has_side_effects=True),
    )(jnp.broadcast_to(wanted[None, :], (8, 128)).astype(jnp.int32))
    ids = lax.dynamic_index_in_dim(everyone[:, 0, :], lax.axis_index("code"), 1, keepdims=False)

    current = codebook.reshape(own_blocks, CBLK, feature)
    logsum = None
    for sweep in range(ITERS):
        fetched = pl.pallas_call(
            functools.partial(fetch_kernel, n_code),
            out_shape=jax.ShapeDtypeStruct((n_code, CBLK, feature), f32),
            in_specs=[SM, VM],
            out_specs=VM,
            scratch_shapes=[
                pltpu.VMEM((n_code, CBLK, feature), f32), dma((n_code,)), dma((n_code,))
            ],
            compiler_params=pltpu.CompilerParams(
                collective_id=1 + 2 * sweep, has_side_effects=True, vmem_limit_bytes=VLIMIT
            ),
        )(ids, current)
        sums, logsum = pl.pallas_call(
            functools.partial(assign_kernel, n_code, key_blocks, block, feature),
            out_shape=(
                jax.ShapeDtypeStruct((n_code, CBLK + MROWS, feature), f32),
                jax.ShapeDtypeStruct((key_blocks, 1, block), f32),
            ),
            in_specs=[SM, SM, VM, VM],
            out_specs=(VM, VM),
            scratch_shapes=[
                pltpu.VMEM((n_code, CBLK, 512), jnp.bfloat16),
                pltpu.VMEM((512, block), jnp.bfloat16),
                pltpu.VMEM((block, 256), jnp.bfloat16),
                pltpu.VMEM((LIST_MAX, CBLK, block), f32),
                pltpu.VMEM((n_code, CBLK, 256), f32),
                pltpu.VMEM((8, block), f32),
            ],
            compiler_params=pltpu.CompilerParams(vmem_limit_bytes=VLIMIT),
        )(slots, counts, fetched, cached_keys)
        n_y = n_dp // 2
        gathered = pl.pallas_call(
            functools.partial(gather_kernel, n_dp, n_code),
            out_shape=jax.ShapeDtypeStruct((n, CBLK + MROWS, feature), f32),
            in_specs=[VM],
            out_specs=VM,
            scratch_shapes=[
                dma((n_code,)), dma((n_code,)),
                dma((n_y, n_code)), dma((n_y, n_code)),
                dma((n_y, n_code)), dma((n_y, n_code)),
                dma,
            ],
            compiler_params=pltpu.CompilerParams(
                collective_id=2 + 2 * sweep, has_side_effects=True, vmem_limit_bytes=VLIMIT
            ),
        )(sums)
        current = pl.pallas_call(
            functools.partial(update_kernel, n, own_blocks),
            out_shape=jax.ShapeDtypeStruct((own_blocks, CBLK, feature), f32),
            in_specs=[SM, VM, VM],
            out_specs=VM,
            scratch_shapes=[
                pltpu.VMEM((own_blocks, CBLK, feature), f32),
                pltpu.VMEM((own_blocks, MROWS, feature), f32),
            ],
            compiler_params=pltpu.CompilerParams(vmem_limit_bytes=VLIMIT),
        )(ids, gathered, current)
    return (current.reshape(own_rows, feature), logsum.reshape(-1))


def solution(mesh):
    in_specs = (
        P(("dp", "code"), None),
        P("code", None),
        P(("dp", "code"), None),
        P(("dp", "code")),
    )
    out_specs = (P("code", None), P(("dp", "code")))
    return jax.shard_map(
        on_device, mesh=mesh, in_specs=in_specs, out_specs=out_specs, check_vma=False
    )
```

time: 560 us -> 241 us (0.43)
  Pallas kernels: 0 us -> 235 us
  waiting for transfers between devices: 199 us -> 0 us
  other arithmetic: 104 us -> 0.8 us
  local copies, waits for them, and re-layouts: 76.7 us -> 2.96 us
  matrix products: 68.6 us -> 0 us
  blocking collectives: 61.1 us -> 0 us
  starting transfers between devices: 32 us -> 0 us
  between operations: 14.7 us -> 0.69 us
    pallas_call x0 -> x9, Pallas kernels: none -> 235 us  [the longest x2 93.8 us: on_device(): pl.pallas_call(functools.partial(gather_kernel, n_dp, n_code), out_shape=...]
    all_to_all x7 -> x0, waiting for transfers between devices: 87.6 us -> none  [the longest x2 48.5 us: serve_blocks(): lax.all_to_all(served, 'code', split_axis=0, concat_axis=0, tiled=True)]
    dot_general x32 -> x0, matrix products: 68.6 us -> none  [the longest x16 45 us: one_block(): lax.dot_general(tile_keys.astype(jnp.float32), word_rows, (((1,), (1,)),...]
    all_gather x2 -> x0, waiting for transfers between devices: 68.4 us -> none  [on_device(): current = lax.all_gather(updated, 'dp', axis=0, tiled=True)]
    scatter-add x36 -> x0, other arithmetic: 66.4 us -> none  [the longest x16 48.6 us: one_block(): slot_sums.at[slot_picks].add(weighted.reshape(LIST_MAX, CBLK, feature))]
    gather x38 -> x0, local copies, waits for them, and re-layouts: 48 us -> none  [the longest x16 29.1 us: one_block(): word_rows = fetched[slot_picks].reshape(-1, feature)]
    reduce_scatter x2 -> x0, waiting for transfers between devices: 42.7 us -> none  [on_device(): lax.psum_scatter(owner_sums, 'dp', scatter_dimension=0, tiled=True)]
    all_to_all x2 -> x0, blocking collectives: 39.3 us -> none  [the longest x1 29.4 us: on_device(): lax.all_to_all(slot_sums.reshape(code_count, CAP, CBLK, feature), 'code',...]
  transfers between devices with their start and end apart: 11 -> 0, of which waited for: 11 -> 0; matrix products, arithmetic and copies ran while one was open for 3% -> 0% of each run, Pallas kernels for 0% -> 0%
where the time goes in v1:
time: 241 us; the launch traced here: 239 us
  Pallas kernels  235 us (98%)
  local copies, waits for them, and re-layouts  2.96 us (1%)
    pallas_call x2, Pallas kernels, on_device(): pl.pallas_call(functools.partial(gather_kernel, n_dp, n_code), out_shape=...  93.8 us
    pallas_call x2, Pallas kernels, on_device(): pl.pallas_call(functools.partial(assign_kernel, n_code, key_blocks, block...  58.5 us
    pallas_call x2, Pallas kernels, on_device(): pl.pallas_call(functools.partial(fetch_kernel, n_code), out_shape=jax.Sha...  49.6 us
    pallas_call x2, Pallas kernels, on_device(): pl.pallas_call(functools.partial(update_kernel, n, own_blocks), out_shape...  19.7 us
    pallas_call x1, Pallas kernels, on_device(): pl.pallas_call(functools.partial(ids_kernel, n_dp, n_code), out_shape=jax...  13.2 us

profile of v1, /device:TPU:0, one launch (start us, length us, event | category | flops | bytes accessed | tf_op | source)
XLA Modules:
  0.0 239.2 jit_solution(8862811042202469933)
XLA Ops:
  0.6 0.7 add_select_fusion.1
  1.3 0.0 copy-start
  1.3 0.1 broadcast_in_dim.21
  1.4 0.1 eq.17
  1.5 0.1 select_reduce_fusion
  1.6 0.6 broadcast_in_dim.24.want_ref
  2.2 13.2 %shard_map.59 = s32[32,8,128]{2,1,0:T(8,128)} custom-call(s32[8,128]{1,0:T(8,128)} %broadcast_in_dim.24.want_ref), custom_call_target="tpu_custom_call" | custom-call | tf_op jit(solution)/shard_map/pallas_call | solution.py:305
  15.4 0.9 slice.3
  16.3 1.3 dynamic-slice_reduce_fusion.ids_ref
  17.6 23.7 %shard_map.60.fetched_ref = f32[8,256,128]{2,1,0:T(8,128)} custom-call(s32[32]{0:T(128)} %dynamic-slice_reduce_fusion.ids_ref, f32[32,256,128]{2,1,0:T(8,128)} %bitcast.3), custom_call_target="tpu_custom_call" | custom-call | tf_op jit(solution)/shard_map/pallas_call | solution.py:318
  41.3 0.0 copy-done
  41.3 29.2 %shard_map.61 = (f32[8,264,128]{2,1,0:T(8,128)}, f32[8,1,512]{2,1,0:T(1,128)}) custom-call(s32[8,6]{1,0:T(8,128)} %copy-done, s32[8]{0:T(128)} %counts_ref.3, f32[8,256,128]{2,1,0:T(8,128)} %shard_map.60.fetched_ref, bf16[4096,128]{1,0:T(8,128)(2,1)} %keys_ref.3), custom_call_target="tpu_custom_call" | custom-call | tf_op jit(solution)/shard_map/pallas_call | solution.py:330
  70.5 45.8 %shard_map.62.con_ref = f32[32,264,128]{2,1,0:T(8,128)} custom-call(f32[8,264,128]{2,1,0:T(8,128)} %get-tuple-element.5.sums_ref), custom_call_target="tpu_custom_call" | custom-call | tf_op jit(solution)/shard_map/pallas_call | solution.py:349
  116.3 9.8 %shard_map.63.book_ref = f32[32,256,128]{2,1,0:T(8,128)} custom-call(s32[32]{0:T(128)} %dynamic-slice_reduce_fusion.ids_ref, f32[32,264,128]{2,1,0:T(8,128)} %shard_map.62.con_ref, f32[32,256,128]{2,1,0:T(8,128)} %bitcast.4), custom_call_target="tpu_custom_call" | custom-call | tf_op jit(solution)/shard_map/pallas_call | solution.py:364
  126.1 25.9 %shard_map.64.fetched_ref = f32[8,256,128]{2,1,0:T(8,128)} custom-call(s32[32]{0:T(128)} %dynamic-slice_reduce_fusion.ids_ref, f32[32,256,128]{2,1,0:T(8,128)} %shard_map.63.book_ref), custom_call_target="tpu_custom_call" | custom-call | tf_op jit(solution)/shard_map/pallas_call | solution.py:318
  152.0 29.2 %shard_map.65 = (f32[8,264,128]{2,1,0:T(8,128)}, f32[8,1,512]{2,1,0:T(1,128)}) custom-call(s32[8,6]{1,0:T(8,128)} %copy-done, s32[8]{0:T(128)} %counts_ref.3, f32[8,256,128]{2,1,0:T(8,128)} %shard_map.64.fetched_ref, bf16[4096,128]{1,0:T(8,128)(2,1)} %keys_ref.3), custom_call_target="tpu_custom_call" | custom-call | tf_op jit(solution)/shard_map/pallas_call | solution.py:330
  181.2 48.0 %shard_map.66.con_ref = f32[32,264,128]{2,1,0:T(8,128)} custom-call(f32[8,264,128]{2,1,0:T(8,128)} %get-tuple-element.6.sums_ref), custom_call_target="tpu_custom_call" | custom-call | tf_op jit(solution)/shard_map/pallas_call | solution.py:349
  229.3 9.9 %shard_map.67 = f32[32,256,128]{2,1,0:T(8,128)} custom-call(s32[32]{0:T(128)} %dynamic-slice_reduce_fusion.ids_ref, f32[32,264,128]{2,1,0:T(8,128)} %shard_map.66.con_ref, f32[32,256,128]{2,1,0:T(8,128)} %shard_map.63.book_ref), custom_call_target="tpu_custom_call" | custom-call | tf_op jit(solution)/shard_map/pallas_call | solution.py:364
Async XLA Ops:
  1.3 39.9 %copy-start = (s32[8,6]{1,0:T(8,128)}, s32[8,6]{1,0:T(8,128)S(1)}, u32[]{:S(2)}) copy-start(s32[8,6]{1,0:T(8,128)S(1)} %get-tuple-element.8.slots_ref) | copy-start | bytes 580

commit v2 on v1

v2 whole, which is shorter than its diff:
```python
import functools
import math

import jax
import jax.numpy as jnp
from jax import lax
from jax.experimental import pallas as pl
from jax.experimental.pallas import tpu as pltpu
from jax.sharding import PartitionSpec as P

CBLK = 256
LIST_MAX = 6
ITERS = 2
MROWS = 8
MESH = pl.DeviceIdType.MESH
VLIMIT = 60 * 1024 * 1024
HELD_BYTES = 16 * 1024 * 1024

VM = pl.BlockSpec(memory_space=pltpu.VMEM)
SM = pl.BlockSpec(memory_space=pltpu.SMEM)
ANY = pl.BlockSpec(memory_space=pl.ANY)


def flip(value, bits):
    out = value
    bit = 1
    while bit <= bits:
        if bits & bit:
            out = out + bit * (1 - 2 * (value // bit % 2))
        bit *= 2
    return out


def remote(src, dst, send, recv, dp, code):
    return pltpu.make_async_remote_copy(
        src_ref=src, dst_ref=dst, send_sem=send, recv_sem=recv,
        device_id=(dp, code), device_id_type=MESH,
    )


def fetch_kernel(
    n_code, want_ref, book_hbm, out_ref, served_ref, asked_ref,
    book, ids, id_send, id_recv, send_sem, recv_sem, book_sem, own_sem, smem_sem,
):
    d = lax.axis_index("dp")
    o = lax.axis_index("code")
    barrier = pltpu.get_barrier_semaphore()
    for k in range(1, n_code):
        pl.semaphore_signal(barrier, inc=1, device_id=(d, flip(o, k)), device_id_type=MESH)
    load = pltpu.make_async_copy(book_hbm, book, book_sem)
    load.start()
    own = pltpu.make_async_copy(want_ref.at[o], asked_ref.at[o], own_sem)
    own.start()
    pl.semaphore_wait(barrier, n_code - 1)
    asks = []
    for k in range(1, n_code):
        peer = flip(o, k)
        copy = remote(
            want_ref.at[peer], asked_ref.at[o], id_send.at[k], id_recv.at[k], d, peer
        )
        copy.start()
        asks.append(copy)
    load.wait()
    copies = []
    for k in range(1, n_code):
        peer = flip(o, k)
        asks[k - 1].wait_recv()
        move = pltpu.make_async_copy(asked_ref.at[peer], ids.at[k], smem_sem.at[k])
        move.start()
        move.wait()
        served_ref[peer] = book[ids[k, 0, 0]]
        copy = remote(
            served_ref.at[peer], out_ref.at[o], send_sem.at[k], recv_sem.at[k], d, peer
        )
        copy.start()
        copies.append(copy)
    own.wait()
    move = pltpu.make_async_copy(asked_ref.at[o], ids.at[0], smem_sem.at[0])
    move.start()
    move.wait()
    block = book[ids[0, 0, 0]]
    served_ref[o] = block
    out_ref[o] = block
    for ask in asks:
        ask.wait_send()
    for copy in copies:
        copy.wait()


def exchange_kernel(n_dp, n_code, reply, *refs):
    if reply:
        (sums_ref, served_ref, asked_ref, con_ref, back_ref, acc, stage,
         a_send, a_recv, y_send, y_recv, c_send, c_recv, own_sem, b_send, b_recv) = refs
    else:
        (sums_ref, con_ref,
         a_send, a_recv, y_send, y_recv, c_send, c_recv, own_sem) = refs
    d = lax.axis_index("dp")
    o = lax.axis_index("code")
    n_y = n_dp // 2
    y = d // 2
    core = d % 2
    mate = y * 2 + 1 - core
    barrier = pltpu.get_barrier_semaphore()
    for k in range(1, n_code):
        pl.semaphore_signal(barrier, inc=1, device_id=(d, flip(o, k)), device_id_type=MESH)
    for j in range(1, n_y):
        pl.semaphore_signal(
            barrier, inc=1, device_id=((y + j) % n_y * 2 + core, o), device_id_type=MESH
        )
    pl.semaphore_signal(barrier, inc=1, device_id=(mate, o), device_id_type=MESH)
    own = pltpu.make_async_copy(sums_ref.at[o], con_ref.at[d * n_code + o], own_sem)
    own.start()
    pl.semaphore_wait(barrier, n_code - 1 + n_y - 1 + 1)

    sends = []
    across = []
    for k in range(1, n_code):
        peer = flip(o, k)
        copy = remote(
            sums_ref.at[peer], con_ref.at[d * n_code + o], a_send.at[k], a_recv.at[k], d, peer
        )
        copy.start()
        across.append(copy)
        sends.append(copy)

    def to_y(k, j):
        row = d * n_code + flip(o, k)
        return remote(
            con_ref.at[row], con_ref.at[row], y_send.at[j, k], y_recv.at[j, k],
            (y + j) % n_y * 2 + core, o,
        )

    def held(k, j):
        return ((y + n_y - j) % n_y * 2 + core) * n_code + flip(o, k)

    def to_mate(k, j):
        row = held(k, j)
        return remote(
            con_ref.at[row], con_ref.at[row], c_send.at[j, k], c_recv.at[j, k], mate, o
        )

    if reply:
        acc[...] = jnp.zeros_like(acc)

    def absorb(row):
        if not reply:
            return
        here = con_ref[row, pl.ds(CBLK + 2, 1), :]

        def one(i, c):
            same = (asked_ref[i, pl.ds(0, 1), :].astype(jnp.float32) == here).astype(jnp.float32)
            acc[i] += con_ref[row] * same
            return c

        lax.fori_loop(0, n_code, one, 0)

    y_copies = {}
    mates = {}
    for k in range(n_code):
        if k == 0:
            own.wait()
        else:
            across[k - 1].wait_recv()
        for j in range(1, n_y):
            copy = to_y(k, j)
            copy.start()
            y_copies[j, k] = copy
            sends.append(copy)
        copy = to_mate(k, 0)
        copy.start()
        mates[0, k] = copy
        sends.append(copy)
        absorb(held(k, 0))
    for k in range(n_code):
        for j in range(1, n_y):
            y_copies[j, k].wait_recv()
            copy = to_mate(k, j)
            copy.start()
            mates[j, k] = copy
            sends.append(copy)
            absorb(held(k, j))
    for k in range(n_code):
        for j in range(n_y):
            mates[j, k].wait_recv()
            absorb(held(k, j) + (1 - 2 * core) * n_code)
    if reply:
        backs = []
        for k in range(n_code):
            peer = flip(o, k)
            for h in range(2):
                inv = 1.0 / (acc[peer, pl.ds(CBLK + h, 1), :] + 1.0)
                column = jnp.transpose(jnp.broadcast_to(inv, (128, 128)))
                rows = pl.ds(h * 128, 128)
                fresh = (acc[peer, rows, :] + served_ref[peer, rows, :]) * column
                if k == 0:
                    back_ref[o, rows, :] = fresh
                else:
                    stage[k, rows, :] = fresh
        for k in range(n_code - 1, 0, -1):
            copy = remote(
                stage.at[k], back_ref.at[o], b_send.at[k], b_recv.at[k], d, flip(o, k)
            )
            copy.start()
            backs.append(copy)
        for copy in backs:
            copy.wait()
    for copy in sends:
        copy.wait_send()


def finish_kernel(
    n, own_blocks, sweeps, *refs
):
    con_hbm = refs[:sweeps]
    book_hbm, out_hbm = refs[sweeps : sweeps + 2]
    con, total, ids, con_sem, book_sem, out_sem = refs[sweeps + 2 :]
    book = pltpu.make_async_copy(book_hbm, total.at[:, pl.ds(0, CBLK), :], book_sem)
    book.start()
    half = n // 2

    def load(t, h):
        rows = pl.ds(h * half, half)
        return pltpu.make_async_copy(con_hbm[t].at[rows], con.at[rows], con_sem.at[h])

    load(0, 0).start()
    load(0, 1).start()
    book.wait()
    for t in range(sweeps):
        total[:, CBLK:, :] = jnp.ones((own_blocks, MROWS, 128), jnp.float32)
        for h in range(2):
            load(t, h).wait()

            def add(j, c):
                if t == 0:
                    ids[j] = con_ids(con, j)
                b = ids[j]
                total[b] += con[j]
                return c

            lax.fori_loop(h * half, (h + 1) * half, add, 0)
            if t + 1 < sweeps:
                load(t + 1, h).start()

        def scale(b, c):
            for h in range(2):
                inv = 1.0 / total[b, pl.ds(CBLK + h, 1), :]
                column = jnp.transpose(jnp.broadcast_to(inv, (128, 128)))
                rows = pl.ds(h * 128, 128)
                total[b, rows, :] = total[b, rows, :] * column
            return c

        lax.fori_loop(0, own_blocks, scale, 0)
    out = pltpu.make_async_copy(total.at[:, pl.ds(0, CBLK), :], out_hbm, out_sem)
    out.start()
    out.wait()


def con_ids(con, j):
    return jnp.max(con[j, pl.ds(CBLK + 2, 1), :]).astype(jnp.int32)


def assign_kernel(
    n_slots, key_blocks, block, feature,
    slots_ref, counts_ref, fetched_ref, keys_ref, want_ref,
    sums_ref, logsum_ref,
    words, norms, kst, kext, scores, acc, top,
):
    inv_scale = 1.0 / math.sqrt(feature)
    log2e = math.log2(math.e)

    def prepare(s, c):
        value = fetched_ref[s]
        hi = value.astype(jnp.bfloat16)
        words[s, :, 0:128] = hi
        words[s, :, 128:256] = (value - hi.astype(jnp.float32)).astype(jnp.bfloat16)
        half = 0.5 * jnp.sum(value * value, axis=1, keepdims=True)
        norms[s] = jnp.broadcast_to(half, (CBLK, 128))
        acc[s] = jnp.zeros((CBLK, 256), jnp.float32)
        return c

    lax.fori_loop(0, n_slots, prepare, 0)
    kext[:, 128:256] = jnp.ones((block, 128), jnp.bfloat16)

    def key_block(kb, c):
        keys = keys_ref[pl.ds(pl.multiple_of(kb * block, block), block), :]
        kext[:, 0:128] = keys
        turned = jnp.transpose(keys)
        kst[0:128, :] = turned
        kst[128:256, :] = turned
        count = counts_ref[kb]
        top[...] = jnp.full((8, block), -3e38, jnp.float32)

        def score(l, c2):
            slot = slots_ref[kb, l]
            s = jnp.dot(words[slot], kst[...], preferred_element_type=jnp.float32)
            s = s - jnp.tile(norms[slot], (1, block // 128))
            scores[l] = s
            top[...] = jnp.maximum(top[...], jnp.max(s.reshape(CBLK // 8, 8, block), axis=0))
            return c2

        lax.fori_loop(0, count, score, 0)
        peak = jnp.max(top[...], axis=0, keepdims=True)

        def expo(l, total):
            e = jnp.exp2((scores[l] - peak) * (inv_scale * log2e))
            scores[l] = e
            return total + jnp.sum(e.reshape(CBLK // 8, 8, block), axis=0)

        total = lax.fori_loop(0, count, expo, jnp.zeros((8, block), jnp.float32))
        total = jnp.sum(total, axis=0, keepdims=True)
        logsum_ref[kb] = peak * inv_scale + jnp.log(total)
        inv = 1.0 / total

        def spread(l, c2):
            p = (scores[l] * inv).astype(jnp.bfloat16)
            slot = slots_ref[kb, l]
            acc[slot] += jnp.dot(p, kext[...], preferred_element_type=jnp.float32)
            return c2

        lax.fori_loop(0, count, spread, 0)
        return c

    lax.fori_loop(0, key_blocks, key_block, 0)

    def write(s, c):
        sums_ref[s, :CBLK, :] = acc[s, :, 0:128]
        for h in range(2):
            turned = jnp.transpose(acc[s, pl.ds(h * 128, 128), pl.ds(128, 128)])
            sums_ref[s, pl.ds(CBLK + h, 1), :] = turned[0:1, :]
        sums_ref[s, CBLK + 2 :, :] = want_ref[s, 2:, :].astype(jnp.float32)
        return c

    lax.fori_loop(0, n_slots, write, 0)


def on_device(cached_keys, codebook, block_lists, counts):
    n_dp = lax.axis_size("dp")
    n_code = lax.axis_size("code")
    n = n_dp * n_code
    own_rows, feature = codebook.shape
    own_blocks = own_rows // CBLK
    key_blocks = block_lists.shape[0]
    block = cached_keys.shape[0] // key_blocks
    f32 = jnp.float32
    dma = pltpu.SemaphoreType.DMA

    slots = block_lists // own_blocks
    local = block_lists % own_blocks
    wanted = jnp.max(
        jnp.where(
            slots.reshape(-1)[:, None] == jnp.arange(128)[None, :], local.reshape(-1)[:, None], 0
        ),
        axis=0,
    )
    want = jnp.broadcast_to(wanted[:n_code, None, None], (n_code, 8, 128)).astype(jnp.int32)
    blocks = jax.ShapeDtypeStruct((n_code, CBLK, feature), f32)
    sums_shape = jax.ShapeDtypeStruct((n_code, CBLK + MROWS, feature), f32)
    con_shape = jax.ShapeDtypeStruct((n, CBLK + MROWS, feature), f32)
    n_y = n_dp // 2

    def params(**kw):
        return pltpu.CompilerParams(vmem_limit_bytes=VLIMIT, **kw)

    book = codebook.reshape(own_blocks, CBLK, feature)
    fetched, served, asked = pl.pallas_call(
        functools.partial(fetch_kernel, n_code),
        out_shape=(blocks, blocks, jax.ShapeDtypeStruct((n_code, 8, 128), jnp.int32)),
        in_specs=[VM, ANY],
        out_specs=(VM, VM, VM),
        scratch_shapes=[
            pltpu.VMEM((own_blocks, CBLK, feature), f32),
            pltpu.SMEM((n_code, 8, 128), jnp.int32),
            dma((n_code,)), dma((n_code,)), dma((n_code,)), dma((n_code,)),
            dma, dma, dma((n_code,)),
        ],
        compiler_params=params(collective_id=0, has_side_effects=True),
    )(want, book)
    logsum = None
    gathered = []
    current = book
    joint = ITERS * n * (CBLK + MROWS) * feature * 4 <= HELD_BYTES

    def finish(parts, held):
        return pl.pallas_call(
            functools.partial(finish_kernel, n, own_blocks, len(parts)),
            out_shape=jax.ShapeDtypeStruct((own_blocks, CBLK, feature), f32),
            in_specs=[ANY] * (len(parts) + 1),
            out_specs=ANY,
            scratch_shapes=[
                pltpu.VMEM(con_shape.shape, f32),
                pltpu.VMEM((own_blocks, CBLK + MROWS, feature), f32),
                pltpu.SMEM((n,), jnp.int32),
                dma((2,)), dma, dma,
            ],
            compiler_params=params(),
        )(*parts, held)

    for sweep in range(ITERS):
        sums, logsum = pl.pallas_call(
            functools.partial(assign_kernel, n_code, key_blocks, block, feature),
            out_shape=(sums_shape, jax.ShapeDtypeStruct((key_blocks, 1, block), f32)),
            in_specs=[SM, SM, VM, VM, VM],
            out_specs=(VM, VM),
            scratch_shapes=[
                pltpu.VMEM((n_code, CBLK, 256), jnp.bfloat16),
                pltpu.VMEM((n_code, CBLK, 128), f32),
                pltpu.VMEM((256, block), jnp.bfloat16),
                pltpu.VMEM((block, 256), jnp.bfloat16),
                pltpu.VMEM((LIST_MAX, CBLK, block), f32),
                pltpu.VMEM((n_code, CBLK, 256), f32),
                pltpu.VMEM((8, block), f32),
            ],
            compiler_params=params(),
        )(slots, counts, fetched, cached_keys, want)
        reply = sweep + 1 < ITERS
        sems = [
            dma((n_code,)), dma((n_code,)),
            dma((n_y, n_code)), dma((n_y, n_code)),
            dma((n_y, n_code)), dma((n_y, n_code)),
            dma,
        ]
        if reply:
            con, fetched = pl.pallas_call(
                functools.partial(exchange_kernel, n_dp, n_code, True),
                out_shape=(con_shape, blocks),
                in_specs=[VM, VM, VM],
                out_specs=(VM, VM),
                scratch_shapes=[
                    pltpu.VMEM(sums_shape.shape, f32), pltpu.VMEM(blocks.shape, f32)
                ] + sems + [dma((n_code,)), dma((n_code,))],
                compiler_params=params(collective_id=1 + sweep, has_side_effects=True),
            )(sums, served, asked)
        else:
            con = pl.pallas_call(
                functools.partial(exchange_kernel, n_dp, n_code, False),
                out_shape=con_shape,
                in_specs=[VM],
                out_specs=VM,
                scratch_shapes=sems,
                compiler_params=params(collective_id=1 + sweep, has_side_effects=True),
            )(sums)
        gathered.append(con)
        if not joint:
            current = finish(gathered, current)
            gathered = []
            if reply:
                current, fetched = lax.optimization_barrier((current, fetched))
    if gathered:
        current = finish(gathered, current)
    return (current.reshape(own_rows, feature), logsum.reshape(-1))


def solution(mesh):
    in_specs = (
        P(("dp", "code"), None),
        P("code", None),
        P(("dp", "code"), None),
        P(("dp", "code")),
    )
    out_specs = (P("code", None), P(("dp", "code")))
    return jax.shard_map(
        on_device, mesh=mesh, in_specs=in_specs, out_specs=out_specs, check_vma=False
    )
```

time: 241 us -> 206 us (0.85)
  Pallas kernels: 235 us -> 202 us
    pallas_call x7 -> x4, Pallas kernels: 176 us -> 157 us  [the longest x1 68 us: on_device(): pl.pallas_call(functools.partial(exchange_kernel, n_dp, n_code, True), ou...]
    pallas_call x2, Pallas kernels: 58.5 us -> 44.8 us  [on_device(): pl.pallas_call(functools.partial(assign_kernel, n_code, key_blocks, block...]
where the time goes in v2:
time: 206 us; the launch traced here: 204 us
  Pallas kernels  202 us (98%)
    pallas_call x1, Pallas kernels, on_device(): pl.pallas_call(functools.partial(exchange_kernel, n_dp, n_code, True), ou...  68 us
    pallas_call x2, Pallas kernels, on_device(): pl.pallas_call(functools.partial(assign_kernel, n_code, key_blocks, block...  44.8 us
    pallas_call x1, Pallas kernels, on_device(): pl.pallas_call(functools.partial(exchange_kernel, n_dp, n_code, False), o...  39 us
    pallas_call x1, Pallas kernels, on_device(): pl.pallas_call(functools.partial(fetch_kernel, n_code), out_shape=(blocks...  33 us
    pallas_call x1, Pallas kernels, finish(): pl.pallas_call(functools.partial(finish_kernel, n, own_blocks, len(parts)...  16.8 us

profile of v2, /device:TPU:0, one launch (start us, length us, event | category | flops | bytes accessed | tf_op | source)
XLA Modules:
  0.0 203.8 jit_solution(10287674711010296285)
XLA Ops:
  0.6 0.7 add_select_fusion
  1.3 0.0 copy-start
  1.3 0.1 broadcast_in_dim.21
  1.4 0.1 eq.17
  1.5 0.1 select_reduce_fusion
  1.6 0.7 broadcast_in_dim.24.want_ref
  2.3 33.0 %shard_map.59 = (f32[8,256,128]{2,1,0:T(8,128)}, f32[8,256,128]{2,1,0:T(8,128)}, s32[8,8,128]{2,1,0:T(8,128)}) custom-call(s32[8,8,128]{2,1,0:T(8,128)} %broadcast_in_dim.24.want_ref, f32[32,256,128]{2,1,0:T(8,128)} %bitcast.4), custom_call_target="tpu_custom_call" | custom-call | tf_op jit(solution)/shard_map/pallas_call | solution.py:365
  35.3 0.0 copy-done
  35.3 22.4 %shard_map.60 = (f32[8,264,128]{2,1,0:T(8,128)}, f32[8,1,512]{2,1,0:T(1,128)}) custom-call(s32[8,6]{1,0:T(8,128)} %copy-done, s32[8]{0:T(128)} %counts_ref.3, f32[8,256,128]{2,1,0:T(8,128)} %get-tuple-element.10.fetched_ref, bf16[4096,128]{1,0:T(8,128)(2,1)} %keys_ref.3, s32[8,8,128]{2,1,0:T(8,128)} %broadcast_in_dim.24.want_ref), custom_call_target="tpu_custom_call" | custom-call | tf_op jit(solution)/shard_map/pallas_call | solution.py:399
  57.7 68.0 %shard_map.61 = (f32[32,264,128]{2,1,0:T(8,128)}, f32[8,256,128]{2,1,0:T(8,128)}) custom-call(f32[8,264,128]{2,1,0:T(8,128)} %get-tuple-element.11.refs_0_, f32[8,256,128]{2,1,0:T(8,128)} %get-tuple-element.12.refs_1_, s32[8,8,128]{2,1,0:T(8,128)} %get-tuple-element.13.refs_2_), custom_call_target="tpu_custom_call" | custom-call | tf_op jit(solution)/shard_map/pallas_call | solution.py:423
  125.6 22.4 %shard_map.62 = (f32[8,264,128]{2,1,0:T(8,128)}, f32[8,1,512]{2,1,0:T(1,128)}) custom-call(s32[8,6]{1,0:T(8,128)} %copy-done, s32[8]{0:T(128)} %counts_ref.3, f32[8,256,128]{2,1,0:T(8,128)} %get-tuple-element.15.fetched_ref, bf16[4096,128]{1,0:T(8,128)(2,1)} %keys_ref.3, s32[8,8,128]{2,1,0:T(8,128)} %broadcast_in_dim.24.want_ref), custom_call_target="tpu_custom_call" | custom-call | tf_op jit(solution)/shard_map/pallas_call | solution.py:399
  148.0 39.0 %shard_map.63.refs_1_ = f32[32,264,128]{2,1,0:T(8,128)} custom-call(f32[8,264,128]{2,1,0:T(8,128)} %get-tuple-element.16.refs_0_), custom_call_target="tpu_custom_call" | custom-call | tf_op jit(solution)/shard_map/pallas_call | solution.py:434
  187.1 16.8 %shard_map.64 = f32[32,256,128]{2,1,0:T(8,128)} custom-call(f32[32,264,128]{2,1,0:T(8,128)} %get-tuple-element.14.refs_0_, f32[32,264,128]{2,1,0:T(8,128)} %shard_map.63.refs_1_, f32[32,256,128]{2,1,0:T(8,128)} %bitcast.5), custom_call_target="tpu_custom_call" | custom-call | tf_op jit(solution)/shard_map/pallas_call | solution.py:384
Async XLA Ops:
  1.3 33.9 %copy-start = (s32[8,6]{1,0:T(8,128)}, s32[8,6]{1,0:T(8,128)S(1)}, u32[]{:S(2)}) copy-start(s32[8,6]{1,0:T(8,128)S(1)} %get-tuple-element.19.slots_ref) | copy-start | bytes 580

commit v3 on v2

--- a/solution.py
+++ b/solution.py
@@ -179,8 +179,10 @@
             mates[j, k] = copy
             sends.append(copy)
             absorb(held(k, j))
+        mates[0, k].wait_recv()
+        absorb(held(k, 0) + (1 - 2 * core) * n_code)
     for k in range(n_code):
-        for j in range(n_y):
+        for j in range(1, n_y):
             mates[j, k].wait_recv()
             absorb(held(k, j) + (1 - 2 * core) * n_code)
     if reply:
@@ -208,13 +210,11 @@
         copy.wait_send()
 
 
-def finish_kernel(
-    n, own_blocks, sweeps, *refs
-):
+def finish_kernel(n, own_blocks, sweeps, *refs):
     con_hbm = refs[:sweeps]
     book_hbm, out_hbm = refs[sweeps : sweeps + 2]
-    con, total, ids, con_sem, book_sem, out_sem = refs[sweeps + 2 :]
-    book = pltpu.make_async_copy(book_hbm, total.at[:, pl.ds(0, CBLK), :], book_sem)
+    con, total, mass, ids, con_sem, book_sem, out_sem = refs[sweeps + 2 :]
+    book = pltpu.make_async_copy(book_hbm, total, book_sem)
     book.start()
     half = n // 2
 
@@ -224,61 +224,66 @@
 
     load(0, 0).start()
     load(0, 1).start()
-    book.wait()
+    outs = []
     for t in range(sweeps):
-        total[:, CBLK:, :] = jnp.ones((own_blocks, MROWS, 128), jnp.float32)
+        mass[...] = jnp.ones_like(mass)
         for h in range(2):
             load(t, h).wait()
+            if t == 0:
+
+                def name(j, c):
+                    for u in range(4):
+                        i = j * 4 + u
+                        ids[i] = jnp.max(con[i, pl.ds(CBLK + 2, 1), :]).astype(jnp.int32)
+                    return c
+
+                lax.fori_loop(h * half // 4, (h + 1) * half // 4, name, 0)
+                if h == 0:
+                    book.wait()
 
             def add(j, c):
-                if t == 0:
-                    ids[j] = con_ids(con, j)
                 b = ids[j]
-                total[b] += con[j]
+                total[b] += con[j, :CBLK, :]
+                for g in range(2):
+                    row = pl.ds(g * (mass.shape[0] // 2) + b, 1)
+                    mass[row, :] += con[j, pl.ds(CBLK + g, 1), :]
                 return c
 
             lax.fori_loop(h * half, (h + 1) * half, add, 0)
             if t + 1 < sweeps:
                 load(t + 1, h).start()
-
-        def scale(b, c):
-            for h in range(2):
-                inv = 1.0 / total[b, pl.ds(CBLK + h, 1), :]
-                column = jnp.transpose(jnp.broadcast_to(inv, (128, 128)))
-                rows = pl.ds(h * 128, 128)
-                total[b, rows, :] = total[b, rows, :] * column
-            return c
-
-        lax.fori_loop(0, own_blocks, scale, 0)
-    out = pltpu.make_async_copy(total.at[:, pl.ds(0, CBLK), :], out_hbm, out_sem)
-    out.start()
-    out.wait()
-
-
-def con_ids(con, j):
-    return jnp.max(con[j, pl.ds(CBLK + 2, 1), :]).astype(jnp.int32)
+        columns = jnp.transpose(1.0 / mass[...])
+        for b in range(own_blocks):
+            for g in range(2):
+                lane = g * (mass.shape[0] // 2) + b
+                total[b, g * 128 : (g + 1) * 128, :] = (
+                    total[b, g * 128 : (g + 1) * 128, :] * columns[:, lane : lane + 1]
+                )
+            if t + 1 == sweeps:
+                out = pltpu.make_async_copy(total.at[b], out_hbm.at[b], out_sem.at[b])
+                out.start()
+                outs.append(out)
+    for out in outs:
+        out.wait()
 
 
 def assign_kernel(
     n_slots, key_blocks, block, feature,
     slots_ref, counts_ref, fetched_ref, keys_ref, want_ref,
     sums_ref, logsum_ref,
-    words, norms, kst, kext, scores, acc, top,
+    words, norms, kst, kext, picked, scores, post, acc,
 ):
-    inv_scale = 1.0 / math.sqrt(feature)
-    log2e = math.log2(math.e)
-
-    def prepare(s, c):
+    scale = math.log2(math.e) / math.sqrt(feature)
+
+    for s in range(n_slots):
         value = fetched_ref[s]
-        hi = value.astype(jnp.bfloat16)
+        scaled = value * scale
+        hi = scaled.astype(jnp.bfloat16)
         words[s, :, 0:128] = hi
-        words[s, :, 128:256] = (value - hi.astype(jnp.float32)).astype(jnp.bfloat16)
-        half = 0.5 * jnp.sum(value * value, axis=1, keepdims=True)
+        words[s, :, 128:256] = (scaled - hi.astype(jnp.float32)).astype(jnp.bfloat16)
+        half = (0.5 * scale) * jnp.sum(value * value, axis=1, keepdims=True)
         norms[s] = jnp.broadcast_to(half, (CBLK, 128))
         acc[s] = jnp.zeros((CBLK, 256), jnp.float32)
-        return c
-
-    lax.fori_loop(0, n_slots, prepare, 0)
     kext[:, 128:256] = jnp.ones((block, 128), jnp.bfloat16)
 
     def key_block(kb, c):
@@ -288,49 +293,41 @@
         kst[0:128, :] = turned
         kst[128:256, :] = turned
         count = counts_ref[kb]
-        top[...] = jnp.full((8, block), -3e38, jnp.float32)
-
-        def score(l, c2):
-            slot = slots_ref[kb, l]
-            s = jnp.dot(words[slot], kst[...], preferred_element_type=jnp.float32)
-            s = s - jnp.tile(norms[slot], (1, block // 128))
-            scores[l] = s
-            top[...] = jnp.maximum(top[...], jnp.max(s.reshape(CBLK // 8, 8, block), axis=0))
-            return c2
-
-        lax.fori_loop(0, count, score, 0)
-        peak = jnp.max(top[...], axis=0, keepdims=True)
-
-        def expo(l, total):
-            e = jnp.exp2((scores[l] - peak) * (inv_scale * log2e))
-            scores[l] = e
-            return total + jnp.sum(e.reshape(CBLK // 8, 8, block), axis=0)
-
-        total = lax.fori_loop(0, count, expo, jnp.zeros((8, block), jnp.float32))
+        slots = [slots_ref[kb, l] for l in range(LIST_MAX)]
+        for l in range(LIST_MAX):
+            picked[l * CBLK : (l + 1) * CBLK, :] = words[slots[l]]
+        raw = jnp.dot(picked[...], kst[...], preferred_element_type=jnp.float32)
+        top = jnp.full((8, block), -3e38, jnp.float32)
+        for l in range(LIST_MAX):
+            rows = slice(l * CBLK, (l + 1) * CBLK)
+            less = norms[slots[l]] + jnp.where(l < count, 0.0, 1e30)
+            s = raw[rows] - jnp.tile(less, (1, block // 128))
+            scores[rows, :] = s
+            top = jnp.maximum(top, jnp.max(s.reshape(CBLK // 8, 8, block), axis=0))
+        peak = jnp.max(top, axis=0, keepdims=True)
+        total = jnp.zeros((8, block), jnp.float32)
+        for l in range(LIST_MAX):
+            rows = slice(l * CBLK, (l + 1) * CBLK)
+            e = jnp.exp2(scores[rows, :] - peak)
+            scores[rows, :] = e
+            total = total + jnp.sum(e.reshape(CBLK // 8, 8, block), axis=0)
         total = jnp.sum(total, axis=0, keepdims=True)
-        logsum_ref[kb] = peak * inv_scale + jnp.log(total)
+        logsum_ref[kb] = peak * math.log(2.0) + jnp.log(total)
         inv = 1.0 / total
-
-        def spread(l, c2):
-            p = (scores[l] * inv).astype(jnp.bfloat16)
-            slot = slots_ref[kb, l]
-            acc[slot] += jnp.dot(p, kext[...], preferred_element_type=jnp.float32)
-            return c2
-
-        lax.fori_loop(0, count, spread, 0)
+        post[...] = (scores[...] * inv).astype(jnp.bfloat16)
+        weighted = jnp.dot(post[...], kext[...], preferred_element_type=jnp.float32)
+        for l in range(LIST_MAX):
+            acc[slots[l]] += weighted[l * CBLK : (l + 1) * CBLK]
         return c
 
     lax.fori_loop(0, key_blocks, key_block, 0)
 
-    def write(s, c):
+    for s in range(n_slots):
         sums_ref[s, :CBLK, :] = acc[s, :, 0:128]
         for h in range(2):
-            turned = jnp.transpose(acc[s, pl.ds(h * 128, 128), pl.ds(128, 128)])
-            sums_ref[s, pl.ds(CBLK + h, 1), :] = turned[0:1, :]
+            turned = jnp.transpose(acc[s, h * 128 : (h + 1) * 128, 128:256])
+            sums_ref[s, CBLK + h : CBLK + h + 1, :] = turned[0:1, :]
         sums_ref[s, CBLK + 2 :, :] = want_ref[s, 2:, :].astype(jnp.float32)
-        return c
-
-    lax.fori_loop(0, n_slots, write, 0)
 
 
 def on_device(cached_keys, codebook, block_lists, counts):
@@ -388,9 +385,10 @@
             out_specs=ANY,
             scratch_shapes=[
                 pltpu.VMEM(con_shape.shape, f32),
-                pltpu.VMEM((own_blocks, CBLK + MROWS, feature), f32),
+                pltpu.VMEM((own_blocks, CBLK, feature), f32),
+                pltpu.VMEM((max(128, 2 * own_blocks), 128), f32),
                 pltpu.SMEM((n,), jnp.int32),
-                dma((2,)), dma, dma,
+                dma((2,)), dma, dma((own_blocks,)),
             ],
             compiler_params=params(),
         )(*parts, held)
@@ -406,9 +404,10 @@
                 pltpu.VMEM((n_code, CBLK, 128), f32),
                 pltpu.VMEM((256, block), jnp.bfloat16),
                 pltpu.VMEM((block, 256), jnp.bfloat16),
-                pltpu.VMEM((LIST_MAX, CBLK, block), f32),
+                pltpu.VMEM((LIST_MAX * CBLK, 256), jnp.bfloat16),
+                pltpu.VMEM((LIST_MAX * CBLK, block), f32),
+                pltpu.VMEM((LIST_MAX * CBLK, block), jnp.bfloat16),
                 pltpu.VMEM((n_code, CBLK, 256), f32),
-                pltpu.VMEM((8, block), f32),
             ],
             compiler_params=params(),
         )(slots, counts, fetched, cached_keys, want)

time: 206 us -> 185 us (0.90)
  Pallas kernels: 202 us -> 182 us
    pallas_call x1, Pallas kernels: 16.8 us -> 8.87 us  [finish(): pl.pallas_call(functools.partial(finish_kernel, n, own_blocks, len(parts)...]
    pallas_call x2, Pallas kernels: 44.8 us -> 38.1 us  [on_device(): pl.pallas_call(functools.partial(assign_kernel, n_code, key_blocks, block...]
    pallas_call x1, Pallas kernels: 68 us -> 64.8 us  [on_device(): pl.pallas_call(functools.partial(exchange_kernel, n_dp, n_code, True), ou...]
where the time goes in v3:
time: 185 us
  Pallas kernels  182 us (98%)
    pallas_call x1, Pallas kernels, on_device(): pl.pallas_call(functools.partial(exchange_kernel, n_dp, n_code, True), ou...  64.8 us
    pallas_call x2, Pallas kernels, on_device(): pl.pallas_call(functools.partial(assign_kernel, n_code, key_blocks, block...  38.1 us
    pallas_call x1, Pallas kernels, on_device(): pl.pallas_call(functools.partial(exchange_kernel, n_dp, n_code, False), o...  37.6 us
    pallas_call x1, Pallas kernels, on_device(): pl.pallas_call(functools.partial(fetch_kernel, n_code), out_shape=(blocks...  33 us
    pallas_call x1, Pallas kernels, finish(): pl.pallas_call(functools.partial(finish_kernel, n, own_blocks, len(parts)...  8.87 us

profile of v3, /device:TPU:0, one launch (start us, length us, event | category | flops | bytes accessed | tf_op | source)
XLA Modules:
  0.0 184.7 jit_solution(4614460482314235039)
XLA Ops:
  0.6 0.7 add_select_fusion
  1.3 0.0 copy-start
  1.3 0.1 broadcast_in_dim.21
  1.4 0.1 eq.17
  1.5 0.1 select_reduce_fusion
  1.6 0.7 broadcast_in_dim.24.want_ref
  2.3 33.0 %shard_map.59 = (f32[8,256,128]{2,1,0:T(8,128)}, f32[8,256,128]{2,1,0:T(8,128)}, s32[8,8,128]{2,1,0:T(8,128)}) custom-call(s32[8,8,128]{2,1,0:T(8,128)} %broadcast_in_dim.24.want_ref, f32[32,256,128]{2,1,0:T(8,128)} %bitcast.4), custom_call_target="tpu_custom_call" | custom-call | tf_op jit(solution)/shard_map/pallas_call | solution.py:362
  35.3 0.0 copy-done
  35.3 19.1 %shard_map.60 = (f32[8,264,128]{2,1,0:T(8,128)}, f32[8,1,512]{2,1,0:T(1,128)}) custom-call(s32[8,6]{1,0:T(8,128)} %copy-done, s32[8]{0:T(128)} %counts_ref.3, f32[8,256,128]{2,1,0:T(8,128)} %get-tuple-element.10.fetched_ref, bf16[4096,128]{1,0:T(8,128)(2,1)} %keys_ref.3, s32[8,8,128]{2,1,0:T(8,128)} %broadcast_in_dim.24.want_ref), custom_call_target="tpu_custom_call" | custom-call | tf_op jit(solution)/shard_map/pallas_call | solution.py:397
  54.3 64.8 %shard_map.61 = (f32[32,264,128]{2,1,0:T(8,128)}, f32[8,256,128]{2,1,0:T(8,128)}) custom-call(f32[8,264,128]{2,1,0:T(8,128)} %get-tuple-element.11.refs_0_, f32[8,256,128]{2,1,0:T(8,128)} %get-tuple-element.12.refs_1_, s32[8,8,128]{2,1,0:T(8,128)} %get-tuple-element.13.refs_2_), custom_call_target="tpu_custom_call" | custom-call | tf_op jit(solution)/shard_map/pallas_call | solution.py:422
  119.1 19.1 %shard_map.62 = (f32[8,264,128]{2,1,0:T(8,128)}, f32[8,1,512]{2,1,0:T(1,128)}) custom-call(s32[8,6]{1,0:T(8,128)} %copy-done, s32[8]{0:T(128)} %counts_ref.3, f32[8,256,128]{2,1,0:T(8,128)} %get-tuple-element.15.fetched_ref, bf16[4096,128]{1,0:T(8,128)(2,1)} %keys_ref.3, s32[8,8,128]{2,1,0:T(8,128)} %broadcast_in_dim.24.want_ref), custom_call_target="tpu_custom_call" | custom-call | tf_op jit(solution)/shard_map/pallas_call | solution.py:397
  138.2 37.6 %shard_map.63.refs_1_ = f32[32,264,128]{2,1,0:T(8,128)} custom-call(f32[8,264,128]{2,1,0:T(8,128)} %get-tuple-element.16.refs_0_), custom_call_target="tpu_custom_call" | custom-call | tf_op jit(solution)/shard_map/pallas_call | solution.py:433
  175.8 8.9 %shard_map.64 = f32[32,256,128]{2,1,0:T(8,128)} custom-call(f32[32,264,128]{2,1,0:T(8,128)} %get-tuple-element.14.refs_0_, f32[32,264,128]{2,1,0:T(8,128)} %shard_map.63.refs_1_, f32[32,256,128]{2,1,0:T(8,128)} %bitcast.5), custom_call_target="tpu_custom_call" | custom-call | tf_op jit(solution)/shard_map/pallas_call | solution.py:381
Async XLA Ops:
  1.3 33.9 %copy-start = (s32[8,6]{1,0:T(8,128)}, s32[8,6]{1,0:T(8,128)S(1)}, u32[]{:S(2)}) copy-start(s32[8,6]{1,0:T(8,128)S(1)} %get-tuple-element.19.slots_ref) | copy-start | bytes 580

commit v4 on v3

--- a/solution.py
+++ b/solution.py
@@ -210,6 +210,236 @@
         copy.wait_send()
 
 
+def fused_kernel(n_dp, n_code, key_blocks, block, feature, reply, *refs):
+    slots_ref, counts_ref, fetched_ref, keys_ref, want_ref = refs[:5]
+    refs = refs[5:]
+    if reply:
+        served_ref, asked_ref, con_ref, logsum_ref, back_ref = refs[:5]
+        refs = refs[5:]
+        acc, stage, b_send, b_recv = refs[:4]
+        refs = refs[4:]
+    else:
+        con_ref, logsum_ref = refs[:2]
+        refs = refs[2:]
+    (words, norms, kst, kext, scores, post, sums, part,
+     a_send, a_recv, y_send, y_recv, c_send, c_recv, own_sem) = refs
+    scale = math.log2(math.e) / math.sqrt(feature)
+    d = lax.axis_index("dp")
+    o = lax.axis_index("code")
+    n_y = n_dp // 2
+    y = d // 2
+    core = d % 2
+    mate = y * 2 + 1 - core
+    barrier = pltpu.get_barrier_semaphore()
+    for k in range(1, n_code):
+        pl.semaphore_signal(barrier, inc=1, device_id=(d, flip(o, k)), device_id_type=MESH)
+    for j in range(1, n_y):
+        pl.semaphore_signal(
+            barrier, inc=1, device_id=((y + j) % n_y * 2 + core, o), device_id_type=MESH
+        )
+    pl.semaphore_signal(barrier, inc=1, device_id=(mate, o), device_id_type=MESH)
+
+    def prepare(s, c):
+        value = fetched_ref[s]
+        scaled = value * scale
+        hi = scaled.astype(jnp.bfloat16)
+        words[s, :, 0:128] = hi
+        words[s, :, 128:256] = (scaled - hi.astype(jnp.float32)).astype(jnp.bfloat16)
+        half = (0.5 * scale) * jnp.sum(value * value, axis=1, keepdims=True)
+        norms[s] = jnp.broadcast_to(half, (CBLK, 128))
+        return c
+
+    lax.fori_loop(0, n_code, prepare, 0)
+    kext[:, 0:128] = keys_ref[...]
+    kext[:, 128:256] = jnp.ones((key_blocks * block, 128), jnp.bfloat16)
+    post[key_blocks * LIST_MAX] = jnp.zeros((CBLK, block), jnp.bfloat16)
+
+    def key_block(kb, c):
+        keys = keys_ref[pl.ds(pl.multiple_of(kb * block, block), block), :]
+        turned = jnp.transpose(keys)
+        kst[0:128, :] = turned
+        kst[128:256, :] = turned
+        count = counts_ref[kb]
+        slots = [slots_ref[kb, l] for l in range(LIST_MAX)]
+        picked = jnp.concatenate([words[slots[l]] for l in range(LIST_MAX)], axis=0)
+        raw = jnp.dot(picked, kst[...], preferred_element_type=jnp.float32)
+        top = jnp.full((8, block), -3e38, jnp.float32)
+        for l in range(LIST_MAX):
+            rows = slice(l * CBLK, (l + 1) * CBLK)
+            less = norms[slots[l]] + jnp.where(l < count, 0.0, 1e30)
+            s = raw[rows] - jnp.tile(less, (1, block // 128))
+            scores[rows, :] = s
+            top = jnp.maximum(top, jnp.max(s.reshape(CBLK // 8, 8, block), axis=0))
+        peak = jnp.max(top, axis=0, keepdims=True)
+        total = jnp.zeros((8, block), jnp.float32)
+        for l in range(LIST_MAX):
+            rows = slice(l * CBLK, (l + 1) * CBLK)
+            e = jnp.exp2(scores[rows, :] - peak)
+            scores[rows, :] = e
+            total = total + jnp.sum(e.reshape(CBLK // 8, 8, block), axis=0)
+        total = jnp.sum(total, axis=0, keepdims=True)
+        logsum_ref[kb] = peak * math.log(2.0) + jnp.log(total)
+        inv = 1.0 / total
+        for l in range(LIST_MAX):
+            rows = slice(l * CBLK, (l + 1) * CBLK)
+            post[kb * LIST_MAX + l] = (scores[rows, :] * inv).astype(jnp.bfloat16)
+        return c
+
+    lax.fori_loop(0, key_blocks, key_block, 0)
+
+    def collect(slot):
+        for kb in range(key_blocks):
+            entry = key_blocks * LIST_MAX
+            for l in range(LIST_MAX):
+                hit = (slots_ref[kb, l] == slot) & (counts_ref[kb] > l)
+                entry = jnp.where(hit, kb * LIST_MAX + l, entry)
+            piece = jnp.dot(
+                post[entry], kext[kb * block : (kb + 1) * block, :],
+                preferred_element_type=jnp.float32,
+            )
+            if kb == 0:
+                part[...] = piece
+            else:
+                part[...] += piece
+        for h in range(2):
+            turned = jnp.transpose(part[h * 128 : (h + 1) * 128, 128:256])
+            sums[slot, CBLK + h : CBLK + h + 1, :] = turned[0:1, :]
+        sums[slot, CBLK + 2 :, :] = want_ref[slot, 2:, :].astype(jnp.float32)
+        sums[slot, :CBLK, :] = part[:, 0:128]
+
+    def turn(k):
+        out = o
+        bit = 1
+        while bit < n_code:
+            out = out + bit * (k // bit % 2) * (1 - 2 * (o // bit % 2))
+            bit *= 2
+        return out
+
+    def across(k):
+        peer = turn(k)
+        return remote(
+            sums.at[peer], con_ref.at[d * n_code + o], a_send.at[k], a_recv.at[k], d, peer
+        )
+
+    far = n_code // 2
+    collect(turn(far))
+    pl.semaphore_wait(barrier, n_code - 1 + n_y - 1 + 1)
+
+    def step(k, c):
+        collect(turn(k))
+        across(k - 1).start()
+        return c
+
+    lax.fori_loop(far + 1, n_code, step, 0)
+    collect(o)
+    across(n_code - 1).start()
+    own = pltpu.make_async_copy(sums.at[o], con_ref.at[d * n_code + o], own_sem)
+    own.start()
+
+    def held(k, j):
+        return ((y + n_y - j) % n_y * 2 + core) * n_code + flip(o, k)
+
+    sends = []
+
+    def to_y(k, j):
+        row = held(k, 0)
+        copy = remote(
+            con_ref.at[row], con_ref.at[row], y_send.at[j, k], y_recv.at[j, k],
+            (y + j) % n_y * 2 + core, o,
+        )
+        copy.start()
+        sends.append(copy)
+        return copy
+
+    def to_mate(k, j):
+        row = held(k, j)
+        copy = remote(
+            con_ref.at[row], con_ref.at[row], c_send.at[j, k], c_recv.at[j, k], mate, o
+        )
+        copy.start()
+        sends.append(copy)
+        return copy
+
+    if reply:
+        acc[...] = jnp.zeros_like(acc)
+
+    def absorb(row):
+        if not reply:
+            return
+        here = con_ref[row, pl.ds(CBLK + 2, 1), :]
+
+        def one(i, c):
+            same = (asked_ref[i, pl.ds(0, 1), :].astype(jnp.float32) == here).astype(jnp.float32)
+            acc[i] += con_ref[row] * same
+            return c
+
+        lax.fori_loop(0, n_code, one, 0)
+
+    y_copies = {}
+    mates = {}
+    own.wait()
+    for j in range(1, n_y):
+        y_copies[j, 0] = to_y(0, j)
+    mates[0, 0] = to_mate(0, 0)
+
+    def near(k, c):
+        collect(turn(k))
+
+        @pl.when(k > 1)
+        def _():
+            across(k - 1).start()
+
+        return c
+
+    lax.fori_loop(1, far, near, 0)
+    absorb(held(0, 0))
+    across(far - 1).start()
+
+    for k in range(1, n_code):
+        across(k).wait_recv()
+        for j in range(1, n_y):
+            y_copies[j, k] = to_y(k, j)
+        mates[0, k] = to_mate(k, 0)
+        absorb(held(k, 0))
+    for k in range(n_code):
+        for j in range(1, n_y):
+            y_copies[j, k].wait_recv()
+            mates[j, k] = to_mate(k, j)
+            absorb(held(k, j))
+        mates[0, k].wait_recv()
+        absorb(held(k, 0) + (1 - 2 * core) * n_code)
+    for k in range(n_code):
+        for j in range(1, n_y):
+            mates[j, k].wait_recv()
+            absorb(held(k, j) + (1 - 2 * core) * n_code)
+    if reply:
+        order = list(range(far, n_code)) + list(range(1, far))
+        for k in order + [0]:
+            peer = flip(o, k)
+            for h in range(2):
+                inv = 1.0 / (acc[peer, pl.ds(CBLK + h, 1), :] + 1.0)
+                column = jnp.transpose(jnp.broadcast_to(inv, (128, 128)))
+                rows = pl.ds(h * 128, 128)
+                fresh = (acc[peer, rows, :] + served_ref[peer, rows, :]) * column
+                if k == 0:
+                    back_ref[o, rows, :] = fresh
+                else:
+                    stage[k, rows, :] = fresh
+        backs = []
+        for k in order:
+            copy = remote(
+                stage.at[k], back_ref.at[o], b_send.at[k], b_recv.at[k], d, flip(o, k)
+            )
+            copy.start()
+            backs.append(copy)
+        for copy in backs:
+            copy.wait()
+    for k in range(1, n_code):
+        across(k).wait_send()
+    for copy in sends:
+        copy.wait_send()
+
+
 def finish_kernel(n, own_blocks, sweeps, *refs):
     con_hbm = refs[:sweeps]
     book_hbm, out_hbm = refs[sweeps : sweeps + 2]
@@ -394,23 +624,6 @@
         )(*parts, held)
 
     for sweep in range(ITERS):
-        sums, logsum = pl.pallas_call(
-            functools.partial(assign_kernel, n_code, key_blocks, block, feature),
-            out_shape=(sums_shape, jax.ShapeDtypeStruct((key_blocks, 1, block), f32)),
-            in_specs=[SM, SM, VM, VM, VM],
-            out_specs=(VM, VM),
-            scratch_shapes=[
-                pltpu.VMEM((n_code, CBLK, 256), jnp.bfloat16),
-                pltpu.VMEM((n_code, CBLK, 128), f32),
-                pltpu.VMEM((256, block), jnp.bfloat16),
-                pltpu.VMEM((block, 256), jnp.bfloat16),
-                pltpu.VMEM((LIST_MAX * CBLK, 256), jnp.bfloat16),
-                pltpu.VMEM((LIST_MAX * CBLK, block), f32),
-                pltpu.VMEM((LIST_MAX * CBLK, block), jnp.bfloat16),
-                pltpu.VMEM((n_code, CBLK, 256), f32),
-            ],
-            compiler_params=params(),
-        )(slots, counts, fetched, cached_keys, want)
         reply = sweep + 1 < ITERS
         sems = [
             dma((n_code,)), dma((n_code,)),
@@ -418,26 +631,78 @@
             dma((n_y, n_code)), dma((n_y, n_code)),
             dma,
         ]
-        if reply:
-            con, fetched = pl.pallas_call(
-                functools.partial(exchange_kernel, n_dp, n_code, True),
-                out_shape=(con_shape, blocks),
-                in_specs=[VM, VM, VM],
+        if joint:
+            ins = [slots, counts, fetched, cached_keys, want]
+            outs = [con_shape, jax.ShapeDtypeStruct((key_blocks, 1, block), f32)]
+            scratch = []
+            if reply:
+                ins += [served, asked]
+                outs += [blocks]
+                scratch = [
+                    pltpu.VMEM(sums_shape.shape, f32), pltpu.VMEM(blocks.shape, f32),
+                    dma((n_code,)), dma((n_code,)),
+                ]
+            scratch += [
+                pltpu.VMEM((n_code, CBLK, 256), jnp.bfloat16),
+                pltpu.VMEM((n_code, CBLK, 128), f32),
+                pltpu.VMEM((256, block), jnp.bfloat16),
+                pltpu.VMEM((key_blocks * block, 256), jnp.bfloat16),
+                pltpu.VMEM((LIST_MAX * CBLK, block), f32),
+                pltpu.VMEM((key_blocks * LIST_MAX + 1, CBLK, block), jnp.bfloat16),
+                pltpu.VMEM(sums_shape.shape, f32),
+                pltpu.VMEM((CBLK, 256), f32),
+            ] + sems
+            results = pl.pallas_call(
+                functools.partial(
+                    fused_kernel, n_dp, n_code, key_blocks, block, feature, reply
+                ),
+                out_shape=tuple(outs),
+                in_specs=[SM, SM] + [VM] * (len(ins) - 2),
+                out_specs=(VM,) * len(outs),
+                scratch_shapes=scratch,
+                compiler_params=params(collective_id=1 + sweep, has_side_effects=True),
+            )(*ins)
+            con, logsum = results[:2]
+            if reply:
+                fetched = results[2]
+        else:
+            sums, logsum = pl.pallas_call(
+                functools.partial(assign_kernel, n_code, key_blocks, block, feature),
+                out_shape=(sums_shape, jax.ShapeDtypeStruct((key_blocks, 1, block), f32)),
+                in_specs=[SM, SM, VM, VM, VM],
                 out_specs=(VM, VM),
                 scratch_shapes=[
-                    pltpu.VMEM(sums_shape.shape, f32), pltpu.VMEM(blocks.shape, f32)
-                ] + sems + [dma((n_code,)), dma((n_code,))],
-                compiler_params=params(collective_id=1 + sweep, has_side_effects=True),
-            )(sums, served, asked)
-        else:
-            con = pl.pallas_call(
-                functools.partial(exchange_kernel, n_dp, n_code, False),
-                out_shape=con_shape,
-                in_specs=[VM],
-                out_specs=VM,
-                scratch_shapes=sems,
-                compiler_params=params(collective_id=1 + sweep, has_side_effects=True),
-            )(sums)
+                    pltpu.VMEM((n_code, CBLK, 256), jnp.bfloat16),
+                    pltpu.VMEM((n_code, CBLK, 128), f32),
+                    pltpu.VMEM((256, block), jnp.bfloat16),
+                    pltpu.VMEM((block, 256), jnp.bfloat16),
+                    pltpu.VMEM((LIST_MAX * CBLK, 256), jnp.bfloat16),
+                    pltpu.VMEM((LIST_MAX * CBLK, block), f32),
+                    pltpu.VMEM((LIST_MAX * CBLK, block), jnp.bfloat16),
+                    pltpu.VMEM((n_code, CBLK, 256), f32),
+                ],
+                compiler_params=params(),
+            )(slots, counts, fetched, cached_keys, want)
+            if reply:
+                con, fetched = pl.pallas_call(
+                    functools.partial(exchange_kernel, n_dp, n_code, True),
+                    out_shape=(con_shape, blocks),
+                    in_specs=[VM, VM, VM],
+                    out_specs=(VM, VM),
+                    scratch_shapes=[
+                        pltpu.VMEM(sums_shape.shape, f32), pltpu.VMEM(blocks.shape, f32)
+                    ] + sems + [dma((n_code,)), dma((n_code,))],
+                    compiler_params=params(collective_id=1 + sweep, has_side_effects=True),
+                )(sums, served, asked)
+            else:
+                con = pl.pallas_call(
+                    functools.partial(exchange_kernel, n_dp, n_code, False),
+                    out_shape=con_shape,
+                    in_specs=[VM],
+                    out_specs=VM,
+                    scratch_shapes=sems,
+                    compiler_params=params(collective_id=1 + sweep, has_side_effects=True),
+                )(sums)
         gathered.append(con)
         if not joint:
             current = finish(gathered, current)

time: 185 us -> 182 us (0.984)
  Pallas kernels: 182 us -> 178 us
    pallas_call x4 -> x2, Pallas kernels: 141 us -> 137 us  [on_device(): pl.pallas_call(functools.partial(fused_kernel, n_dp, n_code, key_blocks,...]
where the time goes in v4:
time: 182 us; the launch traced here: 181 us
  Pallas kernels  178 us (98%)
    pallas_call x2, Pallas kernels, on_device(): pl.pallas_call(functools.partial(fused_kernel, n_dp, n_code, key_blocks,...  137 us
    pallas_call x1, Pallas kernels, on_device(): pl.pallas_call(functools.partial(fetch_kernel, n_code), out_shape=(blocks...  32.9 us
    pallas_call x1, Pallas kernels, finish(): pl.pallas_call(functools.partial(finish_kernel, n, own_blocks, len(parts)...  8.88 us

profile of v4, /device:TPU:0, one launch (start us, length us, event | category | flops | bytes accessed | tf_op | source)
XLA Modules:
  0.0 181.3 jit_solution(13391707991883838121)
XLA Ops:
  0.6 0.7 add_select_fusion
  1.3 0.0 copy-start
  1.3 0.1 broadcast_in_dim.21
  1.4 0.1 eq.17
  1.5 0.1 select_reduce_fusion
  1.6 0.7 broadcast_in_dim.24.want_ref.refs_4_
  2.3 32.9 %shard_map.59 = (f32[8,256,128]{2,1,0:T(8,128)}, f32[8,256,128]{2,1,0:T(8,128)}, s32[8,8,128]{2,1,0:T(8,128)}) custom-call(s32[8,8,128]{2,1,0:T(8,128)} %broadcast_in_dim.24.want_ref.refs_4_, f32[32,256,128]{2,1,0:T(8,128)} %bitcast.4), custom_call_target="tpu_custom_call" | custom-call | tf_op jit(solution)/shard_map/pallas_call | solution.py:592
  35.2 0.0 copy-done
  35.2 77.3 %shard_map.60 = (f32[32,264,128]{2,1,0:T(8,128)}, f32[8,1,512]{2,1,0:T(1,128)}, f32[8,256,128]{2,1,0:T(8,128)}) custom-call(s32[8,6]{1,0:T(8,128)} %copy-done, s32[8]{0:T(128)} %refs_1_.3, f32[8,256,128]{2,1,0:T(8,128)} %get-tuple-element.9.refs_2_, bf16[4096,128]{1,0:T(8,128)(2,1)} %refs_3_.3, s32[8,8,128]{2,1,0:T(8,128)} %broadcast_in_dim.24.want_ref.refs_4_, ...), custom_call_target="tpu_custom_call" | custom-call | tf_op jit(solution)/shard_map/pallas_call | solution.py:655
  112.5 59.3 %shard_map.61 = (f32[32,264,128]{2,1,0:T(8,128)}, f32[8,1,512]{2,1,0:T(1,128)}) custom-call(s32[8,6]{1,0:T(8,128)} %copy-done, s32[8]{0:T(128)} %refs_1_.3, f32[8,256,128]{2,1,0:T(8,128)} %get-tuple-element.13.refs_2_, bf16[4096,128]{1,0:T(8,128)(2,1)} %refs_3_.3, s32[8,8,128]{2,1,0:T(8,128)} %broadcast_in_dim.24.want_ref.refs_4_), custom_call_target="tpu_custom_call" | custom-call | tf_op jit(solution)/shard_map/pallas_call | solution.py:655
  171.8 0.0 copy-start.1
  171.8 8.9 %shard_map.62 = f32[32,256,128]{2,1,0:T(8,128)} custom-call(f32[32,264,128]{2,1,0:T(8,128)} %get-tuple-element.12.refs_0_, f32[32,264,128]{2,1,0:T(8,128)} %get-tuple-element.14.refs_1_, f32[32,256,128]{2,1,0:T(8,128)} %bitcast.5), custom_call_target="tpu_custom_call" | custom-call | tf_op jit(solution)/shard_map/pallas_call | solution.py:611
  180.7 0.0 copy-done.1
  180.7 0.6 copy.7
Async XLA Ops:
  1.3 33.9 %copy-start = (s32[8,6]{1,0:T(8,128)}, s32[8,6]{1,0:T(8,128)S(1)}, u32[]{:S(2)}) copy-start(s32[8,6]{1,0:T(8,128)S(1)} %get-tuple-element.17.refs_0_) | copy-start | bytes 580
  171.8 8.9 %copy-start.1 = (f32[8,1,512]{2,1,0:T(1,128)S(1)}, f32[8,1,512]{2,1,0:T(1,128)}, u32[]{:S(2)}) copy-start(f32[8,1,512]{2,1,0:T(1,128)} %get-tuple-element.15) | copy-start | bytes 49156

commit v5 on v4

--- a/solution.py
+++ b/solution.py
@@ -61,26 +61,31 @@
         copy.start()
         asks.append(copy)
     load.wait()
+    moves = []
+    own.wait()
+    for k in range(n_code):
+        if k > 0:
+            asks[k - 1].wait_recv()
+        move = pltpu.make_async_copy(asked_ref.at[flip(o, k)], ids.at[k], smem_sem.at[k])
+        move.start()
+        moves.append(move)
+    for move in moves:
+        move.wait()
+    order = list(range(n_code // 2, n_code)) + list(range(n_code // 2))
+    for k in order:
+        block = book[ids[k, 0, 0]]
+        served_ref[flip(o, k)] = block
+        if k == 0:
+            out_ref[o] = block
     copies = []
-    for k in range(1, n_code):
-        peer = flip(o, k)
-        asks[k - 1].wait_recv()
-        move = pltpu.make_async_copy(asked_ref.at[peer], ids.at[k], smem_sem.at[k])
-        move.start()
-        move.wait()
-        served_ref[peer] = book[ids[k, 0, 0]]
-        copy = remote(
-            served_ref.at[peer], out_ref.at[o], send_sem.at[k], recv_sem.at[k], d, peer
-        )
-        copy.start()
-        copies.append(copy)
-    own.wait()
-    move = pltpu.make_async_copy(asked_ref.at[o], ids.at[0], smem_sem.at[0])
-    move.start()
-    move.wait()
-    block = book[ids[0, 0, 0]]
-    served_ref[o] = block
-    out_ref[o] = block
+    for k in order:
+        if k > 0:
+            peer = flip(o, k)
+            copy = remote(
+                served_ref.at[peer], out_ref.at[o], send_sem.at[k], recv_sem.at[k], d, peer
+            )
+            copy.start()
+            copies.append(copy)
     for ask in asks:
         ask.wait_send()
     for copy in copies:
@@ -322,19 +327,8 @@
         )
 
     far = n_code // 2
-    collect(turn(far))
+    collect(o)
     pl.semaphore_wait(barrier, n_code - 1 + n_y - 1 + 1)
-
-    def step(k, c):
-        collect(turn(k))
-        across(k - 1).start()
-        return c
-
-    lax.fori_loop(far + 1, n_code, step, 0)
-    collect(o)
-    across(n_code - 1).start()
-    own = pltpu.make_async_copy(sums.at[o], con_ref.at[d * n_code + o], own_sem)
-    own.start()
 
     def held(k, j):
         return ((y + n_y - j) % n_y * 2 + core) * n_code + flip(o, k)
@@ -377,23 +371,26 @@
 
     y_copies = {}
     mates = {}
-    own.wait()
-    for j in range(1, n_y):
-        y_copies[j, 0] = to_y(0, j)
-    mates[0, 0] = to_mate(0, 0)
-
-    def near(k, c):
+    near = list(range(1, far))
+    spread = []
+    for k in range(far, n_code):
+        spread.append(k)
+        if near:
+            spread.append(near.pop(0))
+    for p, k in enumerate(spread):
         collect(turn(k))
-
-        @pl.when(k > 1)
-        def _():
-            across(k - 1).start()
-
-        return c
-
-    lax.fori_loop(1, far, near, 0)
+        if p == 0:
+            own = pltpu.make_async_copy(sums.at[o], con_ref.at[d * n_code + o], own_sem)
+            own.start()
+        else:
+            across(spread[p - 1]).start()
+        if p == 1:
+            own.wait()
+            for j in range(1, n_y):
+                y_copies[j, 0] = to_y(0, j)
+            mates[0, 0] = to_mate(0, 0)
+    across(spread[-1]).start()
     absorb(held(0, 0))
-    across(far - 1).start()
 
     for k in range(1, n_code):
         across(k).wait_recv()

time: 182 us -> 189 us (1.038)
  Pallas kernels: 178 us -> 186 us
    pallas_call x2, Pallas kernels: 137 us -> 145 us  [on_device(): pl.pallas_call(functools.partial(fused_kernel, n_dp, n_code, key_blocks,...]
where the time goes in v5:
time: 189 us
  Pallas kernels  186 us (98%)
    pallas_call x2, Pallas kernels, on_device(): pl.pallas_call(functools.partial(fused_kernel, n_dp, n_code, key_blocks,...  145 us
    pallas_call x1, Pallas kernels, on_device(): pl.pallas_call(functools.partial(fetch_kernel, n_code), out_shape=(blocks...  32.1 us
    pallas_call x1, Pallas kernels, finish(): pl.pallas_call(functools.partial(finish_kernel, n, own_blocks, len(parts)...  8.88 us

profile of v5, /device:TPU:0, one launch (start us, length us, event | category | flops | bytes accessed | tf_op | source)
XLA Modules:
  0.0 188.5 jit_solution(12107719641608840058)
XLA Ops:
  0.6 0.7 add_select_fusion
  1.3 0.0 copy-start
  1.3 0.1 broadcast_in_dim.21
  1.4 0.1 eq.17
  1.5 0.1 select_reduce_fusion
  1.6 0.7 broadcast_in_dim.24.want_ref.refs_4_
  2.3 32.1 %shard_map.59 = (f32[8,256,128]{2,1,0:T(8,128)}, f32[8,256,128]{2,1,0:T(8,128)}, s32[8,8,128]{2,1,0:T(8,128)}) custom-call(s32[8,8,128]{2,1,0:T(8,128)} %broadcast_in_dim.24.want_ref.refs_4_, f32[32,256,128]{2,1,0:T(8,128)} %bitcast.4), custom_call_target="tpu_custom_call" | custom-call | tf_op jit(solution)/shard_map/pallas_call | solution.py:589
  34.4 0.0 copy-done
  34.4 82.3 %shard_map.60 = (f32[32,264,128]{2,1,0:T(8,128)}, f32[8,1,512]{2,1,0:T(1,128)}, f32[8,256,128]{2,1,0:T(8,128)}) custom-call(s32[8,6]{1,0:T(8,128)} %copy-done, s32[8]{0:T(128)} %refs_1_.3, f32[8,256,128]{2,1,0:T(8,128)} %get-tuple-element.9.refs_2_, bf16[4096,128]{1,0:T(8,128)(2,1)} %refs_3_.3, s32[8,8,128]{2,1,0:T(8,128)} %broadcast_in_dim.24.want_ref.refs_4_, ...), custom_call_target="tpu_custom_call" | custom-call | tf_op jit(solution)/shard_map/pallas_call | solution.py:652
  116.8 62.2 %shard_map.61 = (f32[32,264,128]{2,1,0:T(8,128)}, f32[8,1,512]{2,1,0:T(1,128)}) custom-call(s32[8,6]{1,0:T(8,128)} %copy-done, s32[8]{0:T(128)} %refs_1_.3, f32[8,256,128]{2,1,0:T(8,128)} %get-tuple-element.13.refs_2_, bf16[4096,128]{1,0:T(8,128)(2,1)} %refs_3_.3, s32[8,8,128]{2,1,0:T(8,128)} %broadcast_in_dim.24.want_ref.refs_4_), custom_call_target="tpu_custom_call" | custom-call | tf_op jit(solution)/shard_map/pallas_call | solution.py:652
  179.0 0.0 copy-start.1
  179.0 8.9 %shard_map.62 = f32[32,256,128]{2,1,0:T(8,128)} custom-call(f32[32,264,128]{2,1,0:T(8,128)} %get-tuple-element.12.refs_0_, f32[32,264,128]{2,1,0:T(8,128)} %get-tuple-element.14.refs_1_, f32[32,256,128]{2,1,0:T(8,128)} %bitcast.5), custom_call_target="tpu_custom_call" | custom-call | tf_op jit(solution)/shard_map/pallas_call | solution.py:608
  187.9 0.0 copy-done.1
  187.9 0.6 copy.7
Async XLA Ops:
  1.3 33.1 %copy-start = (s32[8,6]{1,0:T(8,128)}, s32[8,6]{1,0:T(8,128)S(1)}, u32[]{:S(2)}) copy-start(s32[8,6]{1,0:T(8,128)S(1)} %get-tuple-element.17.refs_0_) | copy-start | bytes 580
  179.0 8.9 %copy-start.1 = (f32[8,1,512]{2,1,0:T(1,128)S(1)}, f32[8,1,512]{2,1,0:T(1,128)}, u32[]{:S(2)}) copy-start(f32[8,1,512]{2,1,0:T(1,128)} %get-tuple-element.15) | copy-start | bytes 49156
